TPU v7x, 32 devices: a whole 2x2x4 slice. The times are simulated.
32 devices in a mesh: grp: 2 (over y), tau: 16 (over z, x, core).
Axes of the slice: x: 2, y: 2, z: 4, core: 2. Of those that a mesh axis runs over, the one named last changes fastest.
Arguments:
- propagator: float32 [4096, 36864], P(('grp', 'tau')), parts along dimension 0, may hold values from -2.4 to 2.4, as said below
- onsite_coupling: float32 [2], P('grp'), parts along dimension 0, may hold values from 2 to 4
- neighbour_strength: float32 [2], P('grp'), parts along dimension 0, may hold values from 0.3 to 1
Outputs:
- self_energy: float32 [4096, 36864], P(('grp', 'tau')), parts along dimension 0
There are 2 independent parts, one for each index of `grp`. A program takes and returns all parts, laid end to end along the dimension named above; each array names one. Nothing has to cross between parts.
Inputs may be any that keep to these rules, and one draw needn't show every extreme that they name: propagator is even in the lattice vector: propagator[t, x * 192 + y] equals propagator[t, ((-x) mod 192) * 192 + ((-y) mod 192)].
All inputs are finite; a program needn't handle non-finite values.
Results may differ from a plain program's by a relative error of at most 0.00016.
Values sent between devices are 32-bit elements; how exact they have to be, the bound alone decides.
No kernel may reach another device: no remote copies, remote signals or barrier semaphores. Data moves between devices by JAX's collectives and lax.ppermute only.
A program may use at most 256 MiB of HBM per device.

v0:
```python
import math

import jax
import jax.numpy as jnp
from jax import lax
from jax.sharding import PartitionSpec as P

L = 192
TAU_POINTS = 2048
NF = 1024


largest_mode = lax.Precision.HIGHEST


def time_tables():
    matsubara_frequency = jnp.arange(NF, dtype=jnp.int32)[:, None]
    time_points = jnp.arange(TAU_POINTS, dtype=jnp.int32)[None, :]
    fourier_phase = matsubara_frequency * (2 * time_points + 1) % (2 * TAU_POINTS)
    forward = jnp.cos(jnp.pi * fourier_phase.astype(jnp.float32) / TAU_POINTS) / math.sqrt(
        TAU_POINTS
    )
    inverse = forward * jnp.where(matsubara_frequency == 0, 1.0, 2.0).astype(jnp.float32)
    return (forward, inverse)


def space_tables():
    waves = jnp.arange(L, dtype=jnp.int32)
    fourier_phase = waves[:, None] * waves[None, :] % L
    angle = 2.0 * jnp.pi * fourier_phase.astype(jnp.float32) / L
    return (jnp.cos(angle) / math.sqrt(L), jnp.sin(angle) / math.sqrt(L))


def spatial_transform(field, cosine, sine_table):
    first_cos = jnp.einsum("kx,fxy->fky", cosine, field, precision=largest_mode)
    first_sin = jnp.einsum("kx,fxy->fky", sine_table, field, precision=largest_mode)
    return jnp.einsum("fky,ly->fkl", first_cos, cosine, precision=largest_mode) - jnp.einsum(
        "fky,ly->fkl", first_sin, sine_table, precision=largest_mode
    )


def bare_potential(indices, onsite, nearest):
    first = (indices // L).astype(jnp.float32)
    second = (indices % L).astype(jnp.float32)
    return onsite + 2.0 * nearest * (
        jnp.cos(2.0 * jnp.pi * first / L) + jnp.cos(2.0 * jnp.pi * second / L)
    )


def screen(pol_mom, bare):
    denom = jnp.maximum(1.0 - bare * pol_mom, 1.0)
    return bare * bare * pol_mom / denom


def through_slabs(propagator, mirrored, onsite_coupling, neighbour_strength):
    forward, inverse = time_tables()
    cosine, sine_table = space_tables()
    slab_len = propagator.shape[0]
    lattice_site_count = propagator.shape[1]
    block_len = lattice_site_count // lax.axis_size("tau")
    polarization = -propagator * mirrored
    pol_mom = spatial_transform(polarization.reshape(slab_len, L, L), cosine, sine_table).reshape(
        slab_len, lattice_site_count
    )
    by_momentum = lax.all_to_all(pol_mom, "tau", split_axis=1, concat_axis=0, tiled=True)
    pol_freq = jnp.dot(forward, by_momentum, precision=largest_mode)
    indices = lax.axis_index("tau") * block_len + jnp.arange(block_len, dtype=jnp.int32)
    bare = bare_potential(indices, onsite_coupling[0], neighbour_strength[0])
    screened = screen(pol_freq, bare[None, :])
    w_columns = jnp.dot(inverse.T, screened, precision=largest_mode)
    back_slab = lax.all_to_all(w_columns, "tau", split_axis=0, concat_axis=1, tiled=True)
    w_time = spatial_transform(back_slab.reshape(slab_len, L, L), cosine, sine_table).reshape(
        slab_len, lattice_site_count
    )
    return -propagator * w_time


def per_device(propagator, onsite_coupling, neighbour_strength):
    spread = lax.all_to_all(propagator, "tau", split_axis=1, concat_axis=0, tiled=True)
    mirrored = lax.all_to_all(spread[::-1], "tau", split_axis=0, concat_axis=1, tiled=True)
    return through_slabs(propagator, mirrored, onsite_coupling, neighbour_strength)


def solution(mesh):
    in_specs = (P(("grp", "tau"), None), P("grp"), P("grp"))
    out_specs = P(("grp", "tau"), None)
    return jax.shard_map(
        per_device, mesh=mesh, in_specs=in_specs, out_specs=out_specs, check_vma=False
    )
```

profile of v0, /device:TPU:11, one launch (start us, length us, event | category | flops | bytes accessed | tf_op | source)
XLA Modules:
  0.0 2419.1 jit_solution(3030118865738618266)
XLA Ops:
  0.0 18.6 copy.9
  18.6 413.4 %all_to_all.73 = f32[128,16,2304]{0,2,1:T(8,128)} all-to-all(f32[128,16,2304]{0,2,1:T(8,128)} %bitcast.55), channel_id=1, replica_groups=mesh['grp'=2,'tau'=16] {'tau'}, dimensions={1} | all-to-all | bytes 37748736 | tf_op jit(solution)/shard_map/all_to_all | solution.py:79
  432.0 18.7 copy.11
  450.7 143.7 %rev.3 = f32[2048,2304]{1,0:T(8,128)} reverse(f32[2048,2304]{1,0:T(8,128)} %bitcast.57), dimensions={0} | reverse | bytes 37748736 | tf_op jit(solution)/shard_map/rev | solution.py:80
  594.4 413.5 %all_to_all.74 = f32[16,128,2304]{2,1,0:T(8,128)} all-to-all(f32[16,128,2304]{2,1,0:T(8,128)} %bitcast.58), channel_id=1, replica_groups=mesh['grp'=2,'tau'=16] {'tau'}, dimensions={0} | all-to-all | bytes 37748736 | tf_op jit(solution)/shard_map/all_to_all | solution.py:80
  1007.9 18.7 copy.12
  1026.6 12.4 bitcast_multiply_fusion.1
  1039.1 37.6 %fusion.31 = f32[128,192,192]{0,1,2:T(8,128)} fusion(f32[128,192,192]{0,2,1:T(8,128)S(1)} %bitcast.51), kind=kOutput, calls=%fused_computation.30 | convolution fusion | flops 10872004608 | bytes 37748736 | tf_op jit(solution)/shard_map/kx,fxy->fky/dot_general | solution.py:36
  1076.7 37.7 %fusion.28 = f32[128,192,192]{0,1,2:T(8,128)} fusion(f32[128,192,192]{0,2,1:T(8,128)S(1)} %bitcast.52), kind=kOutput, calls=%fused_computation.29 | convolution fusion | flops 10872004608 | bytes 37748736 | tf_op jit(solution)/shard_map/kx,fxy->fky/dot_general | solution.py:35
  1114.4 37.1 %fusion.4 = f32[128,192,192]{0,2,1:T(8,128)} fusion(f32[128,192,192]{0,1,2:T(8,128)} %fusion.31), kind=kOutput, calls=%fused_computation.6 | convolution fusion | flops 10872004608 | bytes 37748736 | tf_op jit(solution)/shard_map/fky,ly->fkl/dot_general | solution.py:37
  1151.5 39.1 %fusion.22 = f32[128,192,192]{0,2,1:T(8,128)} fusion(f32[128,192,192]{0,2,1:T(8,128)} %fusion.4, f32[128,192,192]{0,1,2:T(8,128)} %fusion.28), kind=kOutput, calls=%fused_computation.27 | convolution fusion | flops 10876723200 | bytes 56623104 | tf_op jit(solution)/shard_map/fky,ly->fkl/dot_general | solution.py:37
  1190.5 18.7 copy.17
  1217.2 32.0 %fusion.171 = f32[1024,2048]{1,0:T(8,128)} fusion(s32[2048]{0:T(1024)S(1)} %multiply_add_fusion), kind=kLoop, calls=%fused_computation.38.clone.1 | loop fusion | flops 31457280 | bytes 8396800 | tf_op jit(solution)/shard_map/dot_general | solution.py:66
  1249.2 373.6 %all-to-all-done.2 = f32[128,16,2304]{2,0,1:T(8,128)} async-done(((f32[128,16,2304]{2,0,1:T(8,128)}), f32[128,16,2304]{2,0,1:T(8,128)}, u32[]{:S(2)}, u32[]{:S(2)}) %all-to-all-start.2) | async-done | bytes 18874400 | tf_op jit(solution)/shard_map/all_to_all | solution.py:65
  1622.8 63.7 %fusion.44 = f32[1024,2304]{1,0:T(8,128)S(1)} fusion(f32[2048,2304]{1,0:T(8,128)} %bitcast.15, f32[1024,2048]{1,0:T(8,128)} %fusion.171), kind=kOutput, calls=%fused_computation.37 | convolution fusion | flops 57982058496 | bytes 36700160 | tf_op jit(solution)/shard_map/dot_general | solution.py:66
  1692.2 106.8 %fusion.16 = f32[2048,2304]{1,0:T(8,128)} fusion(f32[1024]{0:T(1024)S(1)} %select_multiply_fusion, s32[2048]{0:T(1024)S(1)} %multiply_add_fusion, f32[1024,2304]{1,0:T(8,128)} %fusion.169), kind=kOutput, calls=%fused_computation.21 | convolution fusion | flops 58013515776 | bytes 28323840 | tf_op jit(solution)/shard_map/dot_general | solution.py:70
  1798.9 18.7 copy.18
  1817.7 411.6 %all_to_all.75 = f32[16,128,2304]{1,2,0:T(8,128)S(1)} all-to-all(f32[16,128,2304]{1,2,0:T(8,128)} %copy.18), channel_id=1, replica_groups=mesh['grp'=2,'tau'=16] {'tau'}, dimensions={0} | all-to-all | bytes 37748736 | tf_op jit(solution)/shard_map/all_to_all | solution.py:71
  2229.2 37.6 %fusion.37 = f32[128,192,192]{0,1,2:T(8,128)} fusion(f32[128,192,192]{0,2,1:T(8,128)S(1)} %bitcast.53), kind=kOutput, calls=%fused_computation.32 | convolution fusion | flops 10872004608 | bytes 37748736 | tf_op jit(solution)/shard_map/kx,fxy->fky/dot_general | solution.py:36
  2266.8 37.6 %fusion.34 = f32[128,192,192]{0,1,2:T(8,128)} fusion(f32[128,192,192]{0,2,1:T(8,128)S(1)} %bitcast.54), kind=kOutput, calls=%fused_computation.31 | convolution fusion | flops 10872004608 | bytes 37748736 | tf_op jit(solution)/shard_map/kx,fxy->fky/dot_general | solution.py:35
  2304.4 37.1 %fusion = f32[128,192,192]{0,2,1:T(8,128)} fusion(f32[128,192,192]{0,1,2:T(8,128)} %fusion.37), kind=kOutput, calls=%fused_computation.2 | convolution fusion | flops 10872004608 | bytes 37748736 | tf_op jit(solution)/shard_map/fky,ly->fkl/dot_general | solution.py:37
  2341.5 38.9 %fusion.25 = f32[128,192,192]{0,2,1:T(8,128)} fusion(f32[128,192,192]{0,2,1:T(8,128)} %fusion, f32[128,192,192]{0,1,2:T(8,128)} %fusion.34), kind=kOutput, calls=%fused_computation.28 | convolution fusion | flops 10876723200 | bytes 56623104 | tf_op jit(solution)/shard_map/fky,ly->fkl/dot_general | solution.py:37
  2380.4 19.6 bitcast_multiply_fusion
  2400.0 18.6 copy.23
  (5 shorter events, 12.3 us)
Async XLA Ops:
  1209.2 413.7 %all-to-all-start.2 = ((f32[128,16,2304]{2,0,1:T(8,128)}), f32[128,16,2304]{2,0,1:T(8,128)}, u32[]{:S(2)}, u32[]{:S(2)}) async-start(f32[128,16,2304]{2,0,1:T(8,128)} %copy.17), calls=%async_computation.2 | async-start | bytes 37748736 | tf_op jit(solution)/shard_map/all_to_all | solution.py:65
where the time goes:
time: 2440 us; the launch traced here: 2420 us
  blocking collectives  1240 us (51%)
  matrix products  473 us (19%)
  waiting for transfers between devices  374 us (15%)
  local copies, waits for them, and re-layouts  256 us (10%)
  other arithmetic  69.7 us (3%)
    all_to_all x1, blocking collectives, per_device(): lax.all_to_all(spread[::-1], 'tau', split_axis=0, concat_axis=1, tiled=True)  414 us
    all_to_all x1, blocking collectives, per_device(): lax.all_to_all(propagator, 'tau', split_axis=1, concat_axis=0, tiled=True)  413 us
    all_to_all x1, blocking collectives, through_slabs(): lax.all_to_all(w_columns, 'tau', split_axis=0, concat_axis=1, tiled=True)  412 us
    all_to_all x1, waiting for transfers between devices, through_slabs(): lax.all_to_all(pol_mom, 'tau', split_axis=1, concat_axis=0, tiled=True)  374 us
    rev x1, local copies, waits for them, and re-layouts, per_device(): spread[::-1]  144 us
    dot_general x1, matrix products, through_slabs(): w_columns = jnp.dot(inverse.T, screened, precision=largest_mode)  107 us
    dot_general x2, matrix products, spatial_transform(): jnp.einsum('fky,ly->fkl', first_cos, cosine, precision=largest_mode)  77.9 us
    dot_general x2, matrix products, spatial_transform(): first_cos = jnp.einsum('kx,fxy->fky', cosine, field, precision=largest_mode)  75.3 us
  transfers between devices with their start and end apart: 1, of which 1 were waited for; matrix products, arithmetic and copies ran while one was open for 1% of the time, Pallas kernels for 0%

commit v1 on v0

v1 whole, which is shorter than its diff:
```python
import math

import jax
import jax.numpy as jnp
import numpy as np
from jax import lax
from jax.experimental import pallas as pl
from jax.experimental.pallas import tpu as pltpu
from jax.sharding import PartitionSpec as P

L = 192
TAU_POINTS = 2048
NF = 1024

mode = lax.Precision.HIGH


def cos_table(rows, columns, period):
    phase = rows[:, None] * columns[None, :] % period
    return jnp.cos(2.0 * jnp.pi * phase.astype(jnp.float32) / period)


def sin_table(rows, columns, period):
    phase = rows[:, None] * columns[None, :] % period
    return jnp.sin(2.0 * jnp.pi * phase.astype(jnp.float32) / period)


def time_table(times, points):
    frequency = jnp.arange(NF, dtype=jnp.int32)[None, :]
    phase = frequency * (2 * times[:, None] + 1) % (2 * points)
    return jnp.cos(jnp.pi * phase.astype(jnp.float32) / points) / math.sqrt(points)


def bare_potential(first, second, onsite, nearest):
    first = first.astype(jnp.float32)
    second = second.astype(jnp.float32)
    return onsite + 2.0 * nearest * (
        jnp.cos(2.0 * jnp.pi * first / L) + jnp.cos(2.0 * jnp.pi * second / L)
    )


def screen(pol_mom, bare):
    denom = jnp.maximum(1.0 - bare * pol_mom, 1.0)
    return bare * bare * pol_mom / denom


def plain(propagator, onsite_coupling, neighbour_strength):
    devices = lax.axis_size("tau")
    slab, sites = propagator.shape
    half = slab // 2
    points = slab * devices
    kept = L // 2 + 1
    width = kept * L
    block = -(-width // (8 * devices)) * 8
    padded = block * devices

    waves = jnp.arange(L, dtype=jnp.int32)
    halves = jnp.arange(kept, dtype=jnp.int32)
    twice = jnp.where((halves == 0) | (halves == L // 2), 1.0, 2.0).astype(jnp.float32)

    partner = [(d, devices - 1 - d) for d in range(devices)]
    mirrored = lax.ppermute(propagator[half:, :width], "tau", partner)
    polarization = -propagator[:half, :width] * mirrored[::-1]

    field = polarization.reshape(half, kept, L)
    along_cos = cos_table(halves, waves, L) / L
    along_sin = sin_table(halves, waves, L) / L
    first_cos = jnp.einsum("fxy,ly->fxl", field, along_cos, precision=mode)
    first_sin = jnp.einsum("fxy,ly->fxl", field, along_sin, precision=mode)
    cos_x = cos_table(waves, halves, L)
    sin_x = sin_table(waves, halves, L)
    pol_mom = jnp.einsum("fxl,kx->flk", first_cos, cos_x * twice, precision=mode) - jnp.einsum(
        "fxl,kx->flk", first_sin, sin_x * twice, precision=mode
    )
    pol_mom = jnp.pad(pol_mom.reshape(half, width), ((0, 0), (0, padded - width)))
    by_momentum = lax.all_to_all(pol_mom, "tau", split_axis=1, concat_axis=0, tiled=True)

    held = jnp.arange(devices * half, dtype=jnp.int32)
    times = held // half * slab + held % half
    forward = 2.0 * time_table(times, points)
    pol_freq = jnp.einsum("tn,tq->nq", forward, by_momentum, precision=mode)
    momenta = lax.axis_index("tau") * block + jnp.arange(block, dtype=jnp.int32)
    bare = bare_potential(momenta % L, momenta // L, onsite_coupling[0], neighbour_strength[0])
    screened = screen(pol_freq, bare[None, :])
    weight = jnp.where(jnp.arange(NF) == 0, 1.0, 2.0).astype(jnp.float32)
    inverse = time_table(jnp.arange(points, dtype=jnp.int32), points) * weight
    w_columns = jnp.einsum("tn,nq->tq", inverse, screened, precision=mode)

    back = lax.all_to_all(w_columns, "tau", split_axis=0, concat_axis=1, tiled=True)
    back = back[:, :width].reshape(slab, kept, L)
    back_cos = jnp.einsum("flk,kx->flx", back, cos_table(waves, waves, L) / L, precision=mode)
    back_sin = jnp.einsum("flk,kx->flx", back, sin_table(waves, waves, L) / L, precision=mode)
    w_time = jnp.einsum("flx,yl->fxy", back_cos, cos_table(waves, halves, L) * twice, precision=mode) - jnp.einsum(
        "flx,yl->fxy", back_sin, sin_table(waves, halves, L) * twice, precision=mode
    )
    return -propagator * w_time.reshape(slab, sites)


LANES = 128
PAIR = 2 * L
HALF_L = L // 2
KEPT = HALF_L + 1
ROWS_X = 104
Z_ROWS = 216
bf16 = jnp.bfloat16
f32 = jnp.float32
NN = (((1,), (0,)), ((), ()))
NT = (((1,), (1,)), ((), ()))


def halves_of(x):
    high = x.astype(bf16)
    return high, (x - high.astype(f32)).astype(bf16)


def product(a, b, dims):
    return lax.dot_general(a, b, dims, preferred_element_type=f32)


def product3(a, b, dims):
    return product(a[0], b[0], dims) + product(a[0], b[1], dims) + product(a[1], b[0], dims)


def table_halves(table):
    high = np.asarray(table, np.float32).astype(bf16)
    low = (np.asarray(table, np.float64) - high.astype(np.float64)).astype(np.float32).astype(bf16)
    return jnp.asarray(high), jnp.asarray(low)


def np_angle(a, b):
    return 2.0 * np.pi * ((a[:, None] * b[None, :]) % L) / L


def np_twice(a):
    return np.where((a == 0) | (a == HALF_L), 1.0, np.where(a > HALF_L, 0.0, 2.0))


def along_y_table():
    table = np.zeros((256, 512))
    angle = np_angle(np.arange(KEPT), np.arange(L))
    for i, part in enumerate((np.cos(angle), np.sin(angle))):
        table[128 * i : 128 * i + KEPT, 0:L] = part / L
        table[128 * i : 128 * i + KEPT, 256 + 64 : 512] = part / L
    return table_halves(table)


def along_x_table(pairs):
    table = np.zeros((L, 2 * pairs))
    for parity in (0, 1):
        x = 2 * np.arange(pairs) + parity
        angle = np_angle(np.arange(HALF_L), x)
        rows = slice(HALF_L * parity, HALF_L * (parity + 1))
        table[rows, :pairs] = np.cos(angle) * np_twice(x)
        table[rows, pairs:] = -np.sin(angle) * np_twice(x)
    return table_halves(table)


def back_x_table():
    table = np.zeros((2 * ROWS_X, L))
    angle = np_angle(np.arange(KEPT), np.arange(L))
    table[:KEPT] = np.cos(angle) / L
    table[ROWS_X : ROWS_X + KEPT] = np.sin(angle) / L
    return table_halves(table)


def back_y_table():
    table = np.zeros((4, 2 * ROWS_X, 256))
    ky = np.arange(KEPT)
    angle = np_angle(ky, np.arange(L))
    weight = np_twice(ky)[:, None]
    for side in (0, 1):
        for parity in (0, 1):
            columns = slice(64 * parity, 64 * parity + L)
            table[2 * side + parity, :KEPT, columns] = weight * np.cos(angle)
            table[2 * side + parity, ROWS_X : ROWS_X + KEPT, columns] = (
                (2 * side - 1) * weight * np.sin(angle)
            )
    return table_halves(table)


def lane_swap(x):
    return pltpu.roll(x, LANES // 2, 1)


GROUP = 8


def bubble_kernel(limit, own_ref, mirror_ref, flip_ref, high_ref, low_ref, out_ref):
    start = pl.program_id(0) * GROUP
    table = (high_ref[...], low_ref[...])
    flip = flip_ref[...]
    empty = jnp.zeros((64, 256), f32)
    for u in range(GROUP // 2):
        lanes = slice(2 * u * PAIR, (2 * u + 2) * PAIR)
        high, low = halves_of(mirror_ref[:, lanes])
        mirrored = product(flip, high, NN) + product(flip, low, NN)
        bubble = -own_ref[:, lanes] * mirrored
        rows = []
        for v in range(2):
            field = bubble[:, v * PAIR : (v + 1) * PAIR]
            field = jnp.where(start + 2 * u + v < limit, field, 0.0)
            rows.append(jnp.concatenate([field[:, :256], empty], axis=1))
            rows.append(jnp.concatenate([empty, field[:, 128:]], axis=1))
        stacked = jnp.concatenate(rows, axis=0)
        result = product3(table, halves_of(stacked), NT)
        out_ref[2 * u] = result[:, :LANES]
        out_ref[2 * u + 1] = result[:, LANES:]


def bubble_along_y(propagator, mirror, first, pairs):
    half = propagator.shape[0] // 2
    steps = -(-pairs // GROUP)
    shift = first // GROUP
    width = GROUP * PAIR
    high, low = along_y_table()
    flip = jnp.asarray(np.eye(half)[::-1].astype(bf16))
    whole = lambda a: pl.BlockSpec(a.shape, lambda i: (0,) * a.ndim)
    return pl.pallas_call(
        lambda *refs: bubble_kernel(pairs, *refs),
        grid=(steps,),
        in_specs=[
            pl.BlockSpec((half, width), lambda i: (0, i + shift)),
            pl.BlockSpec((half, width), lambda i: (0, i)),
            whole(flip),
            whole(high),
            whole(low),
        ],
        out_specs=pl.BlockSpec((GROUP, 256, LANES), lambda i: (i, 0, 0)),
        out_shape=jax.ShapeDtypeStruct((steps * GROUP, 256, LANES), f32),
        cost_estimate=pl.CostEstimate(
            flops=6 * pairs * 256 * 256 * 256, bytes_accessed=3 * half * pairs * PAIR * 4, transcendentals=0
        ),
        interpret=INTERPRET,
        name="bubble_along_y",
    )(propagator, mirror, flip, high, low)


KY_STEP = 14


def along_x_kernel(counts, *refs):
    parts, (high_ref, low_ref, out_ref) = refs[: len(counts)], refs[len(counts) :]
    table = (high_ref[...], low_ref[...])
    first_half = lax.broadcasted_iota(jnp.int32, (HALF_L, LANES), 1) < LANES // 2

    def lines(ky):
        return jnp.concatenate(
            [
                part[pl.ds(offset + ky, count, stride=256), :]
                for offset in (0, 128)
                for part, count in zip(parts, counts)
            ],
            axis=0,
        )

    first = pl.program_id(0) * KY_STEP

    def body(m, carry):
        ky = first + 2 * m
        both = jnp.concatenate([lines(ky), lines(ky + 1)], axis=1)
        result = product3(table, halves_of(both), NN)
        for v in range(2):
            even = result[:HALF_L, LANES * v : LANES * (v + 1)]
            odd = result[HALF_L:, LANES * v : LANES * (v + 1)]
            out_ref[pl.ds((2 * m + v) * HALF_L, HALF_L), :] = jnp.where(
                first_half, even + lane_swap(odd), lane_swap(even) - odd
            )
        return carry

    lax.fori_loop(0, KY_STEP // 2, body, 0)


def along_x(parts, rows):
    counts = tuple(p.shape[0] for p in parts)
    high, low = along_x_table(sum(counts))
    flat = [p.reshape(-1, LANES) for p in parts]
    whole = lambda a: pl.BlockSpec(a.shape, lambda i: (0,) * a.ndim)
    block = KY_STEP * HALF_L
    return pl.pallas_call(
        lambda *refs: along_x_kernel(counts, *refs),
        grid=(-(-rows // block),),
        in_specs=[whole(a) for a in (*flat, high, low)],
        out_specs=pl.BlockSpec((block, LANES), lambda i: (i, 0)),
        out_shape=jax.ShapeDtypeStruct((rows, LANES), f32),
        cost_estimate=pl.CostEstimate(
            flops=6 * KEPT * L * 256 * LANES, bytes_accessed=12 * 1024 * 1024, transcendentals=0
        ),
        interpret=INTERPRET,
        name="along_x",
    )(*flat, high, low)


def frequency_kernel(side, x_ref, bare_ref, high_ref, low_ref, out_ref):
    sources = x_ref.shape[0]
    first_half = lax.broadcasted_iota(jnp.int32, x_ref.shape[1:], 1) < LANES // 2
    pieces = []
    for k in range(sources // 2):
        near, far = x_ref[k], x_ref[sources - 1 - k]
        if side == 0:
            pieces.append(jnp.where(first_half, near, lane_swap(far)))
        else:
            pieces.append(jnp.where(first_half, lane_swap(near), far))
    table = (high_ref[...], low_ref[...])
    pol = product3(halves_of(jnp.concatenate(pieces, axis=1)), table, NN)
    bare = bare_ref[...]
    screened = bare * bare * pol / jnp.maximum(1.0 - bare * pol, 1.0)
    zero = lax.broadcasted_iota(jnp.int32, screened.shape, 1) == 0
    screened = jnp.where(zero, 0.5 * screened, screened)
    w = product3(halves_of(screened), table, NT)
    for k in range(sources // 2):
        piece = w[:, LANES * k : LANES * (k + 1)]
        out_ref[k] = piece
        out_ref[sources - 1 - k] = piece


ROW_BLOCK = 200


def through_frequencies(x, bare, table, side):
    sources, rows, _ = x.shape
    high, low = table
    whole = lambda a: pl.BlockSpec(a.shape, lambda i: (0,) * a.ndim)
    return pl.pallas_call(
        lambda *refs: frequency_kernel(side, *refs),
        grid=(-(-rows // ROW_BLOCK),),
        in_specs=[
            pl.BlockSpec((sources, ROW_BLOCK, LANES), lambda i: (0, i, 0)),
            pl.BlockSpec((ROW_BLOCK, 1), lambda i: (i, 0)),
            whole(high),
            whole(low),
        ],
        out_specs=pl.BlockSpec((sources, ROW_BLOCK, LANES), lambda i: (0, i, 0)),
        out_shape=jax.ShapeDtypeStruct((sources, rows, LANES), f32),
        cost_estimate=pl.CostEstimate(
            flops=12 * rows * high.shape[0] * high.shape[1],
            bytes_accessed=2 * x.size * 4,
            transcendentals=0,
        ),
        interpret=INTERPRET,
        name="through_frequencies",
    )(x, bare, high, low)


X_STEP = 8


def inverse_kernel(low_ref, high_ref, xh_ref, xl_ref, perm_ref, yh_ref, yl_ref, own_ref, out_ref, z_ref):
    @pl.when(pl.program_id(0) == 0)
    def _():
        z_ref[...] = jnp.zeros_like(z_ref)
        table = (xh_ref[...], xl_ref[...])

        def lines(ky):
            rows = pl.ds(ky * HALF_L, HALF_L)
            return jnp.concatenate([low_ref[rows, :], high_ref[rows, :]], axis=0)

        def put(ky, result):
            z_ref[pl.ds(ky, KEPT, stride=Z_ROWS), :] = result[:KEPT]
            z_ref[pl.ds(ROWS_X + ky, KEPT, stride=Z_ROWS), :] = result[ROWS_X : ROWS_X + KEPT]

        def body(m, carry):
            both = jnp.concatenate([lines(2 * m), lines(2 * m + 1)], axis=1)
            result = product3(table, halves_of(both), NN)
            put(2 * m, result[:, :LANES])
            put(2 * m + 1, result[:, LANES:])
            return carry

        lax.fori_loop(0, KEPT // 2, body, 0)
        put(KEPT - 1, product3(table, halves_of(lines(KEPT - 1)), NN))

    perm = perm_ref[...]
    first = pl.program_id(0) * X_STEP
    for u in range(X_STEP // 2):
        sides = []
        for parity in range(2):
            x = first + 2 * u + parity
            mirror = jnp.where(x > HALF_L, L - x, x)
            case = jnp.where(x > HALF_L, 2, 0) + parity
            lines = halves_of(z_ref[pl.ds(mirror * Z_ROWS, 2 * ROWS_X), :])
            turned = tuple(product(perm, part, NT).astype(bf16) for part in lines)
            sides.append(product3(turned, (yh_ref[case], yl_ref[case]), NN))
        even, odd = sides
        base = u * PAIR
        for start, w in ((0, even[:, :128]), (128, even[:, 128:] + odd[:, :128]), (256, odd[:, 128:])):
            lanes = slice(base + start, base + start + 128)
            out_ref[:, lanes] = -own_ref[:, lanes] * w


def back_to_sites(propagator, lower, upper, perm):
    slab, sites = propagator.shape
    xh, xl = back_x_table()
    yh, yl = back_y_table()
    width = X_STEP * L
    whole = lambda a: pl.BlockSpec(a.shape, lambda i: (0,) * a.ndim)
    moving = pl.BlockSpec((slab, width), lambda i: (0, i))
    return pl.pallas_call(
        inverse_kernel,
        grid=(sites // width,),
        in_specs=[whole(a) for a in (lower, upper, xh, xl, perm, yh, yl)] + [moving],
        out_specs=moving,
        out_shape=jax.ShapeDtypeStruct((slab, sites), f32),
        scratch_shapes=[pltpu.VMEM((KEPT * Z_ROWS, LANES), f32)],
        cost_estimate=pl.CostEstimate(
            flops=10 * L * 128 * 256 * 256, bytes_accessed=2 * propagator.size * 4, transcendentals=0
        ),
        interpret=INTERPRET,
        name="back_to_sites",
    )(lower, upper, xh, xl, perm, yh, yl, propagator)


INTERPRET = False
CUTS = (0, 24, KEPT // 2 + 1)


def with_kernels(propagator, onsite_coupling, neighbour_strength):
    devices = lax.axis_size("tau")
    me = lax.axis_index("tau")
    slab, sites = propagator.shape
    half = slab // 2
    points = slab * devices
    rows = -(-KEPT * HALF_L // (8 * devices)) * 8

    partner = [(d, devices - 1 - d) for d in range(devices)]
    parts = []
    for first, last in zip(CUTS[:-1], CUTS[1:]):
        mirror = lax.ppermute(propagator[half:, first * PAIR : last * PAIR], "tau", partner)
        parts.append(bubble_along_y(propagator, mirror, first, last - first))

    slot = lax.optimization_barrier(jnp.arange(points // 2, dtype=jnp.int32))
    lane = slot % slab
    times = slot - lane + jnp.where(lane < half, lane, slab + half - 1 - lane)
    table = 2.0 * time_table(times, points)
    table_high = lax.reduce_precision(table, 8, 7)
    table = (table_high.astype(bf16), (table - table_high).astype(bf16))

    row = me * rows + jnp.arange(rows, dtype=jnp.int32)
    bare = [
        bare_potential(
            (row % HALF_L + HALF_L * side)[:, None], (row // HALF_L)[:, None], onsite_coupling[0], neighbour_strength[0]
        )
        for side in (0, 1)
    ]
    own_row = jnp.arange(slab, dtype=jnp.int32)
    forth = jnp.where(own_row < half, own_row, slab + half - 1 - own_row)
    back = jnp.where(own_row < half, half + own_row, slab - 1 - own_row)
    source = jnp.where(me < devices // 2, forth, back)
    perm = (source[:, None] == own_row[None, :]).astype(bf16)

    pol_mom = along_x(parts, rows * devices).reshape(devices, rows, LANES)
    by_momentum = lax.all_to_all(pol_mom, "tau", split_axis=0, concat_axis=0, tiled=True)
    returned = []
    for side in (0, 1):
        w = through_frequencies(by_momentum, bare[side], table, side)
        w = lax.all_to_all(w, "tau", split_axis=0, concat_axis=0, tiled=True)
        returned.append(w.reshape(devices * rows, LANES))
    return back_to_sites(propagator, returned[0], returned[1], perm)


def per_device(propagator, onsite_coupling, neighbour_strength):
    fits = propagator.shape[0] == LANES and propagator.shape[1] == L * L
    run = with_kernels if fits else plain
    return run(propagator, onsite_coupling, neighbour_strength)


def solution(mesh):
    in_specs = (P(("grp", "tau"), None), P("grp"), P("grp"))
    out_specs = P(("grp", "tau"), None)
    return jax.shard_map(
        per_device, mesh=mesh, in_specs=in_specs, out_specs=out_specs, check_vma=False
    )
```

time: 2440 us -> 639 us (0.26)
  blocking collectives: 1240 us -> 0 us
  matrix products: 473 us -> 0 us
  local copies, waits for them, and re-layouts: 256 us -> 3.68 us
  Pallas kernels: 0 us -> 117 us
  waiting for transfers between devices: 374 us -> 474 us
  other arithmetic: 69.7 us -> 24.8 us
    all_to_all x3 -> x0, blocking collectives: 1240 us -> none  [the longest x1 414 us: per_device(): lax.all_to_all(spread[::-1], 'tau', split_axis=0, concat_axis=1, tiled=True)]
    dot_general x10 -> x0, matrix products: 473 us -> none  [the longest x1 107 us: through_slabs(): w_columns = jnp.dot(inverse.T, screened, precision=largest_mode)]
    ppermute x0 -> x2, waiting for transfers between devices: none -> 199 us  [with_kernels(): lax.ppermute(propagator[half:, first * PAIR:last * PAIR], 'tau', partner)]
    rev x1 -> x0, local copies, waits for them, and re-layouts: 144 us -> none  [per_device(): spread[::-1]]
    pallas_call x0 -> x6, Pallas kernels: none -> 117 us  [the longest x1 50.6 us: back_to_sites(): pl.pallas_call(inverse_kernel, grid=(sites // width,), in_specs=[whole(a)...]
    all_to_all x1 -> x3, waiting for transfers between devices: 374 us -> 275 us  [the longest x2 192 us: with_kernels(): w = lax.all_to_all(w, 'tau', split_axis=0, concat_axis=0, tiled=True)]
    all_to_all x4 -> x0, local copies, waits for them, and re-layouts: 74.8 us -> none  [the longest x1 18.7 us: per_device(): lax.all_to_all(spread[::-1], 'tau', split_axis=0, concat_axis=1, tiled=True)]
    dot_general x2 -> x0, other arithmetic: 37.6 us -> none  [the longest x1 32 us: through_slabs(): pol_freq = jnp.dot(forward, by_momentum, precision=largest_mode)]
  transfers between devices with their start and end apart: 1 -> 5, of which waited for: 1 -> 5; matrix products, arithmetic and copies ran while one was open for 1% -> 4% of each run, Pallas kernels for 0% -> 3%
where the time goes in v1:
time: 639 us; the launch traced here: 638 us
  waiting for transfers between devices  474 us (74%)
  Pallas kernels  117 us (18%)
  other arithmetic  24.8 us (4%)
  starting transfers between devices  17.5 us (3%)
    ppermute x2, waiting for transfers between devices, with_kernels(): lax.ppermute(propagator[half:, first * PAIR:last * PAIR], 'tau', partner)  199 us
    all_to_all x2, waiting for transfers between devices, with_kernels(): w = lax.all_to_all(w, 'tau', split_axis=0, concat_axis=0, tiled=True)  192 us
    all_to_all x1, waiting for transfers between devices, with_kernels(): lax.all_to_all(pol_mom, 'tau', split_axis=0, concat_axis=0, tiled=True)  82.7 us
    pallas_call x1, Pallas kernels, back_to_sites(): pl.pallas_call(inverse_kernel, grid=(sites // width,), in_specs=[whole(a)...  50.6 us
    pallas_call x2, Pallas kernels, through_frequencies(): pl.pallas_call(lambda *refs: frequency_kernel(side, *refs), grid=(-(-rows...  28.7 us
    pallas_call x1, Pallas kernels, along_x(): pl.pallas_call(lambda *refs: along_x_kernel(counts, *refs), grid=(-(-rows...  21.5 us
    convert_element_type x1, other arithmetic, with_kernels(): table = (table_high.astype(bf16), (table - table_high).astype(bf16))  18.1 us
    pallas_call x2, Pallas kernels, bubble_along_y(): pl.pallas_call(lambda *refs: bubble_kernel(pairs, *refs), grid=(steps,),...  16 us
  transfers between devices with their start and end apart: 5, of which 5 were waited for; matrix products, arithmetic and copies ran while one was open for 4% of the time, Pallas kernels for 3%

profile of v1, /device:TPU:11, one launch (start us, length us, event | category | flops | bytes accessed | tf_op | source)
XLA Modules:
  0.0 637.9 jit_solution(4120511116210574629)
XLA Ops:
  0.0 1.8 slice.6
  1.8 1.9 collective-permute-start
  3.7 1.9 slice.7
  5.6 0.9 collective-permute-start.1
  6.5 153.5 %collective-permute-done.refs_1_ = f32[64,9216]{1,0:T(8,128)} collective-permute-done((f32[64,9216]{1,0:T(8,128)S(1)}, f32[64,9216]{1,0:T(8,128)}, u32[]{:S(2)}, u32[]{:S(2)}) %collective-permute-start) | collective-permute-done | bytes 2359328 | tf_op jit(solution)/shard_map/ppermute | solution.py:426
  160.0 7.3 %bubble_along_y.2 = f32[24,256,128]{2,1,0:T(8,128)} custom-call(f32[128,36864]{1,0:T(8,128)} %own_ref.1, f32[64,9216]{1,0:T(8,128)} %collective-permute-done.refs_1_, bf16[64,64]{1,0:T(8,128)(2,1)} %constant.115.clone.refs_2_, bf16[256,512]{1,0:T(8,128)(2,1)} %constant.113.clone.refs_3_, bf16[256,512]{1,0:T(8,128)(2,1)} %constant.114.clone.refs_4_), custom_call_target="tpu_custom_call" | custom-call | flops 2415919104 | bytes 7077888 | tf_op jit(solution)/shard_map/bubble_along_y/pallas_call | solution.py:218
  167.2 45.4 %collective-permute-done.1.refs_1_ = f32[64,9600]{1,0:T(8,128)} collective-permute-done((f32[64,9600]{1,0:T(8,128)S(1)}, f32[64,9600]{1,0:T(8,128)}, u32[]{:S(2)}, u32[]{:S(2)}) %collective-permute-start.1) | collective-permute-done | bytes 2457632 | tf_op jit(solution)/shard_map/ppermute | solution.py:426
  212.6 8.8 %bubble_along_y.3 = f32[32,256,128]{2,1,0:T(8,128)} custom-call(f32[128,36864]{1,0:T(8,128)} %own_ref.1, f32[64,9600]{1,0:T(8,128)} %collective-permute-done.1.refs_1_, bf16[64,64]{1,0:T(8,128)(2,1)} %constant.115.clone.refs_2_, bf16[256,512]{1,0:T(8,128)(2,1)} %constant.113.clone.refs_3_, bf16[256,512]{1,0:T(8,128)(2,1)} %constant.114.clone.refs_4_), custom_call_target="tpu_custom_call" | custom-call | flops 2516582400 | bytes 7372800 | tf_op jit(solution)/shard_map/bubble_along_y/pallas_call | solution.py:218
  221.4 21.5 %along_x.1 = f32[9344,128]{1,0:T(8,128)} custom-call(f32[6144,128]{1,0:T(8,128)} %bitcast.11, f32[8192,128]{1,0:T(8,128)} %bitcast.10, bf16[192,112]{1,0:T(8,128)(2,1)} %constant.116.clone.refs_2_, bf16[192,112]{1,0:T(8,128)(2,1)} %constant.117.clone.refs_3_), custom_call_target="tpu_custom_call" | custom-call | flops 3661627392 | bytes 12582912 | tf_op jit(solution)/shard_map/along_x/pallas_call | solution.py:279
  242.9 5.2 all-to-all-start
  249.5 3.0 multiply_add_fusion.1.refs_1_
  252.5 18.1 %fusion = (bf16[1024,1024]{1,0:T(8,128)(2,1)}, bf16[1024,1024]{1,0:T(8,128)(2,1)}) fusion(s32[1024]{0:T(1024)S(1)} %fusion.21), kind=kLoop, calls=%fused_computation.5 | loop fusion | flops 19922944 | bytes 4198400 | tf_op jit(solution)/shard_map/convert_element_type | solution.py:434
  270.5 82.7 %all-to-all-done.refs_0_ = f32[16,584,128]{2,1,0:T(8,128)} async-done(((f32[16,584,128]{2,1,0:T(8,128)}), f32[16,584,128]{2,1,0:T(8,128)}, u32[]{:S(2)}, u32[]{:S(2)}) %all-to-all-start) | async-done | bytes 4784160 | tf_op jit(solution)/shard_map/all_to_all | solution.py:450
  353.3 14.4 %through_frequencies.2 = f32[16,584,128]{2,1,0:T(8,128)} custom-call(f32[16,584,128]{2,1,0:T(8,128)} %all-to-all-done.refs_0_, f32[584,1]{1,0:T(8,128)} %multiply_add_fusion.1.refs_1_, bf16[1024,1024]{1,0:T(8,128)(2,1)} %get-tuple-element.6.refs_2_, bf16[1024,1024]{1,0:T(8,128)(2,1)} %get-tuple-element.5.refs_3_), custom_call_target="tpu_custom_call" | custom-call | flops 7348420608 | bytes 9568256 | tf_op jit(solution)/shard_map/through_frequencies/pallas_call | solution.py:323
  367.6 4.7 all-to-all-start.1
  372.4 3.0 multiply_add_fusion.refs_1_
  375.4 14.3 %through_frequencies.3 = f32[16,584,128]{2,1,0:T(8,128)} custom-call(f32[16,584,128]{2,1,0:T(8,128)} %all-to-all-done.refs_0_, f32[584,1]{1,0:T(8,128)} %multiply_add_fusion.refs_1_, bf16[1024,1024]{1,0:T(8,128)(2,1)} %get-tuple-element.6.refs_2_, bf16[1024,1024]{1,0:T(8,128)(2,1)} %get-tuple-element.5.refs_3_), custom_call_target="tpu_custom_call" | custom-call | flops 7348420608 | bytes 9568256 | tf_op jit(solution)/shard_map/through_frequencies/pallas_call | solution.py:323
  389.7 87.8 %all-to-all-done.1 = f32[16,584,128]{2,1,0:T(8,128)} async-done(((f32[16,584,128]{2,1,0:T(8,128)}), f32[16,584,128]{2,1,0:T(8,128)}, u32[]{:S(2)}, u32[]{:S(2)}) %all-to-all-start.1) | async-done | bytes 4784160 | tf_op jit(solution)/shard_map/all_to_all | solution.py:454
  477.5 4.8 all-to-all-start.2
  482.2 0.7 fusion.17.perm_ref
  482.9 104.4 %all-to-all-done.2 = f32[16,584,128]{2,1,0:T(8,128)} async-done(((f32[16,584,128]{2,1,0:T(8,128)}), f32[16,584,128]{2,1,0:T(8,128)}, u32[]{:S(2)}, u32[]{:S(2)}) %all-to-all-start.2) | async-done | bytes 4784160 | tf_op jit(solution)/shard_map/all_to_all | solution.py:454
  587.3 50.6 %back_to_sites.1 = f32[128,36864]{1,0:T(8,128)} custom-call(f32[9344,128]{1,0:T(8,128)} %bitcast.5.low_ref, f32[9344,128]{1,0:T(8,128)} %bitcast.6.high_ref, bf16[208,192]{1,0:T(8,128)(2,1)} %constant.118.clone.xh_ref, bf16[208,192]{1,0:T(8,128)(2,1)} %constant.119.clone.xl_ref, bf16[128,128]{1,0:T(8,128)(2,1)} %fusion.17.perm_ref, ...), custom_call_target="tpu_custom_call" | custom-call | flops 16106127360 | bytes 37748736 | tf_op jit(solution)/shard_map/back_to_sites/pallas_call | solution.py:396
  (3 shorter events, 0.0 us)
Async XLA Ops:
  1.8 158.1 %collective-permute-start = (f32[64,9216]{1,0:T(8,128)S(1)}, f32[64,9216]{1,0:T(8,128)}, u32[]{:S(2)}, u32[]{:S(2)}) collective-permute-start(f32[64,9216]{1,0:T(8,128)S(1)} %slice.6), channel_id=1, source_target_pairs={{0,15},{1,14},{2,13},{3,12},{4,11},{5,10},{6,9},{7,8},{8,7},{9,6},... | collective-permute-start | bytes 7077896 | tf_op jit(solution)/shard_map/ppermute | solution.py:426
  5.6 207.0 %collective-permute-start.1 = (f32[64,9600]{1,0:T(8,128)S(1)}, f32[64,9600]{1,0:T(8,128)}, u32[]{:S(2)}, u32[]{:S(2)}) collective-permute-start(f32[64,9600]{1,0:T(8,128)S(1)} %slice.7), channel_id=1, source_target_pairs={{0,15},{1,14},{2,13},{3,12},{4,11},{5,10},{6,9},{7,8},{8,7},{9,6},... | collective-permute-start | bytes 7372808 | tf_op jit(solution)/shard_map/ppermute | solution.py:426
  242.9 110.3 %all-to-all-start = ((f32[16,584,128]{2,1,0:T(8,128)}), f32[16,584,128]{2,1,0:T(8,128)}, u32[]{:S(2)}, u32[]{:S(2)}) async-start(f32[16,584,128]{2,1,0:T(8,128)} %bitcast.9), calls=%async_computation | async-start | bytes 9568256 | tf_op jit(solution)/shard_map/all_to_all | solution.py:450
  367.6 109.8 %all-to-all-start.1 = ((f32[16,584,128]{2,1,0:T(8,128)}), f32[16,584,128]{2,1,0:T(8,128)}, u32[]{:S(2)}, u32[]{:S(2)}) async-start(f32[16,584,128]{2,1,0:T(8,128)} %through_frequencies.2), calls=%async_computation.1 | async-start | bytes 9568256 | tf_op jit(solution)/shard_map/all_to_all | solution.py:454
  477.5 109.9 %all-to-all-start.2 = ((f32[16,584,128]{2,1,0:T(8,128)}), f32[16,584,128]{2,1,0:T(8,128)}, u32[]{:S(2)}, u32[]{:S(2)}) async-start(f32[16,584,128]{2,1,0:T(8,128)} %through_frequencies.3), calls=%async_computation.2 | async-start | bytes 9568256 | tf_op jit(solution)/shard_map/all_to_all | solution.py:454

commit v2 on v1

v2 whole, which is shorter than its diff:
```python
import math

import jax
import jax.numpy as jnp
import numpy as np
from jax import lax
from jax.experimental import pallas as pl
from jax.experimental.pallas import tpu as pltpu
from jax.sharding import PartitionSpec as P


L = 192
NF = 1024

mode = lax.Precision.HIGH


def cos_table(rows, columns, period):
    phase = rows[:, None] * columns[None, :] % period
    return jnp.cos(2.0 * jnp.pi * phase.astype(jnp.float32) / period)


def sin_table(rows, columns, period):
    phase = rows[:, None] * columns[None, :] % period
    return jnp.sin(2.0 * jnp.pi * phase.astype(jnp.float32) / period)


def time_table(times, points):
    frequency = jnp.arange(NF, dtype=jnp.int32)[None, :]
    phase = frequency * (2 * times[:, None] + 1) % (2 * points)
    return jnp.cos(jnp.pi * phase.astype(jnp.float32) / points) / math.sqrt(points)


def bare_potential(first, second, onsite, nearest):
    first = first.astype(jnp.float32)
    second = second.astype(jnp.float32)
    return onsite + 2.0 * nearest * (
        jnp.cos(2.0 * jnp.pi * first / L) + jnp.cos(2.0 * jnp.pi * second / L)
    )


def screen(pol_mom, bare):
    denom = jnp.maximum(1.0 - bare * pol_mom, 1.0)
    return bare * bare * pol_mom / denom


def plain(propagator, onsite_coupling, neighbour_strength):
    devices = lax.axis_size("tau")
    slab, sites = propagator.shape
    half = slab // 2
    points = slab * devices
    kept = L // 2 + 1
    width = kept * L
    block = -(-width // (8 * devices)) * 8
    padded = block * devices

    waves = jnp.arange(L, dtype=jnp.int32)
    halves = jnp.arange(kept, dtype=jnp.int32)
    twice = jnp.where((halves == 0) | (halves == L // 2), 1.0, 2.0).astype(jnp.float32)

    partner = [(d, devices - 1 - d) for d in range(devices)]
    mirrored = lax.ppermute(propagator[half:, :width], "tau", partner)
    polarization = -propagator[:half, :width] * mirrored[::-1]

    field = polarization.reshape(half, kept, L)
    along_cos = cos_table(halves, waves, L) / L
    along_sin = sin_table(halves, waves, L) / L
    first_cos = jnp.einsum("fxy,ly->fxl", field, along_cos, precision=mode)
    first_sin = jnp.einsum("fxy,ly->fxl", field, along_sin, precision=mode)
    cos_x = cos_table(waves, halves, L)
    sin_x = sin_table(waves, halves, L)
    pol_mom = jnp.einsum("fxl,kx->flk", first_cos, cos_x * twice, precision=mode) - jnp.einsum(
        "fxl,kx->flk", first_sin, sin_x * twice, precision=mode
    )
    pol_mom = jnp.pad(pol_mom.reshape(half, width), ((0, 0), (0, padded - width)))
    by_momentum = lax.all_to_all(pol_mom, "tau", split_axis=1, concat_axis=0, tiled=True)

    held = jnp.arange(devices * half, dtype=jnp.int32)
    times = held // half * slab + held % half
    forward = 2.0 * time_table(times, points)
    pol_freq = jnp.einsum("tn,tq->nq", forward, by_momentum, precision=mode)
    momenta = lax.axis_index("tau") * block + jnp.arange(block, dtype=jnp.int32)
    bare = bare_potential(momenta % L, momenta // L, onsite_coupling[0], neighbour_strength[0])
    screened = screen(pol_freq, bare[None, :])
    weight = jnp.where(jnp.arange(NF) == 0, 1.0, 2.0).astype(jnp.float32)
    inverse = time_table(jnp.arange(points, dtype=jnp.int32), points) * weight
    w_columns = jnp.einsum("tn,nq->tq", inverse, screened, precision=mode)

    back = lax.all_to_all(w_columns, "tau", split_axis=0, concat_axis=1, tiled=True)
    back = back[:, :width].reshape(slab, kept, L)
    back_cos = jnp.einsum("flk,kx->flx", back, cos_table(waves, waves, L) / L, precision=mode)
    back_sin = jnp.einsum("flk,kx->flx", back, sin_table(waves, waves, L) / L, precision=mode)
    w_time = jnp.einsum("flx,yl->fxy", back_cos, cos_table(waves, halves, L) * twice, precision=mode) - jnp.einsum(
        "flx,yl->fxy", back_sin, sin_table(waves, halves, L) * twice, precision=mode
    )
    return -propagator * w_time.reshape(slab, sites)


LANES = 128
PAIR = 2 * L
HALF_L = L // 2
KEPT = HALF_L + 1
ROWS_X = 104
INTERPRET = False
MIB = 1024 * 1024
bf16 = jnp.bfloat16
f32 = jnp.float32
NN = (((1,), (0,)), ((), ()))
NT = (((1,), (1,)), ((), ()))


def halves_of(x):
    high = x.astype(bf16)
    return high, (x - high.astype(f32)).astype(bf16)


def product(a, b, dims):
    return lax.dot_general(a, b, dims, preferred_element_type=f32)


def product3(a, b, dims):
    return product(a[0], b[0], dims) + product(a[0], b[1], dims) + product(a[1], b[0], dims)


def table_halves(table):
    high = np.asarray(table, np.float32).astype(bf16)
    low = (np.asarray(table, np.float64) - high.astype(np.float64)).astype(np.float32).astype(bf16)
    return jnp.asarray(high), jnp.asarray(low)


def np_angle(a, b):
    return 2.0 * np.pi * ((a[:, None] * b[None, :]) % L) / L


def np_twice(a):
    return np.where((a == 0) | (a == HALF_L), 1.0, np.where(a > HALF_L, 0.0, 2.0))


def along_y_table():
    table = np.zeros((256, 512))
    angle = np_angle(np.arange(KEPT), np.arange(L))
    for i, part in enumerate((np.cos(angle), np.sin(angle))):
        table[128 * i : 128 * i + KEPT, 0:L] = part / L
        table[128 * i : 128 * i + KEPT, 256 + 64 : 512] = part / L
    return table_halves(table)


def along_x_table(pairs):
    table = np.zeros((L, 2 * pairs))
    for parity in (0, 1):
        x = 2 * np.arange(pairs) + parity
        angle = np_angle(np.arange(HALF_L), x)
        rows = slice(HALF_L * parity, HALF_L * (parity + 1))
        table[rows, :pairs] = np.cos(angle) * np_twice(x)
        table[rows, pairs:] = -np.sin(angle) * np_twice(x)
    return table_halves(table)


anywhere = pl.BlockSpec(memory_space=pl.ANY)


def lane_swap(x):
    return pltpu.roll(x, LANES // 2, 1)


GROUP = 8


def bubble_kernel(limit, own_ref, mirror_ref, flip_ref, high_ref, low_ref, out_ref):
    start = pl.program_id(0) * GROUP
    table = (high_ref[...], low_ref[...])
    flip = flip_ref[...]
    first_half = lax.broadcasted_iota(jnp.int32, (256, LANES), 1) < LANES // 2
    for u in range(0, GROUP, 4):
        lines = []
        for v in range(u, u + 4, 2):
            lanes = slice(v * PAIR, (v + 2) * PAIR)
            high, low = halves_of(mirror_ref[:, lanes])
            mirrored = product(flip, high, NN) + product(flip, low, NN)
            field = -own_ref[:, lanes] * mirrored
            lines += [field[:, :PAIR], field[:, PAIR:]]
        lines = [jnp.where(start + u + i < limit, line, 0.0) for i, line in enumerate(lines)]
        even = jnp.concatenate([line[:, :256] for line in lines], axis=0)
        odd = jnp.concatenate([line[:, 128:] for line in lines], axis=0)
        even = product3((table[0][:, :256], table[1][:, :256]), halves_of(even), NT)
        odd = product3((table[0][:, 256:], table[1][:, 256:]), halves_of(odd), NT)
        for v in range(2):
            lanes = slice(v * LANES, (v + 1) * LANES)
            near, far = even[:, lanes], odd[:, lanes]
            out_ref[u + 2 * v] = jnp.where(first_half, near, lane_swap(far))
            out_ref[u + 2 * v + 1] = jnp.where(first_half, lane_swap(near), far)


def bubble_along_y(propagator, mirror, first, pairs, before, after):
    half = propagator.shape[0] // 2
    steps = -(-pairs // GROUP)
    shift = first // GROUP
    width = GROUP * PAIR
    high, low = along_y_table()
    flip = jnp.asarray(np.eye(half)[::-1].astype(bf16))
    whole = lambda a: pl.BlockSpec(a.shape, lambda i: (0,) * a.ndim)
    total = -(-(KEPT // 2 + 1) // GROUP) * GROUP
    earlier = [] if before is None else [before]
    return pl.pallas_call(
        lambda *refs: bubble_kernel(pairs, *refs[:5], refs[-1]),
        grid=(steps,),
        in_specs=[
            pl.BlockSpec((half, width), lambda i: (0, i + shift)),
            pl.BlockSpec((half, width), lambda i: (0, i)),
            whole(flip),
            whole(high),
            whole(low),
        ]
        + [anywhere] * (len(earlier) + len(after)),
        out_specs=pl.BlockSpec((GROUP, 256, LANES), lambda i: (i + shift, 0, 0)),
        out_shape=jax.ShapeDtypeStruct((total, 256, LANES), f32),
        input_output_aliases={5: 0} if earlier else {},
        cost_estimate=pl.CostEstimate(
            flops=6 * pairs * 256 * 256 * 256, bytes_accessed=3 * half * pairs * PAIR * 4, transcendentals=0
        ),
        compiler_params=pltpu.CompilerParams(vmem_limit_bytes=16 * MIB),
        interpret=INTERPRET,
        name="bubble_along_y",
    )(propagator, mirror, flip, high, low, *earlier, *after)


def whole(array):
    return pl.BlockSpec(array.shape, lambda *i: (0,) * array.ndim, pipeline_mode=pl.Buffered(1))


def along_x_kernel(first, span, copies, counts, *refs):
    parts, (high_ref, low_ref), out_ref = refs[: len(counts)], refs[len(counts) : len(counts) + 2], refs[-1]
    table = (high_ref[...], low_ref[...])
    first_half = lax.broadcasted_iota(jnp.int32, (HALF_L, LANES), 1) < LANES // 2
    start = first + pl.program_id(0) * span

    def lines(ky):
        return jnp.concatenate(
            [
                part[pl.ds(offset + ky, count, stride=256), :]
                for offset in (0, 128)
                for part, count in zip(parts, counts)
            ],
            axis=0,
        )

    for m in range(0, span, 2):
        both = jnp.concatenate([lines(start + m), lines(start + m + 1)], axis=1)
        result = product3(table, halves_of(both), NN)
        for v in range(2):
            even = result[:HALF_L, LANES * v : LANES * (v + 1)]
            odd = result[HALF_L:, LANES * v : LANES * (v + 1)]
            both_halves = jnp.where(first_half, even + lane_swap(odd), lane_swap(even) - odd)
            for copy in range(copies):
                out_ref[copy, (m + v) * HALF_L : (m + v + 1) * HALF_L, :] = both_halves


def along_x(parts, first, span, rows, copies, after):
    counts = tuple(p.shape[0] for p in parts)
    high, low = along_x_table(sum(counts))
    flat = [p.reshape(-1, LANES) for p in parts]
    block = span * HALF_L
    return pl.pallas_call(
        lambda *refs: along_x_kernel(first, span, copies, counts, *refs),
        grid=(-(-rows // block),),
        in_specs=[whole(a) for a in (*flat, high, low)] + [anywhere] * len(after),
        out_specs=pl.BlockSpec((copies, block, LANES), lambda i: (0, i, 0)),
        out_shape=jax.ShapeDtypeStruct((copies, rows, LANES), f32),
        cost_estimate=pl.CostEstimate(
            flops=6 * rows * 2 * 256 * LANES, bytes_accessed=12 * 1024 * 1024, transcendentals=0
        ),
        compiler_params=pltpu.CompilerParams(vmem_limit_bytes=20 * MIB),
        interpret=INTERPRET,
        name="along_x",
    )(*flat, high, low, *after)


def gathered(x, lane):
    return jnp.take_along_axis(x, lane, axis=1, mode="promise_in_bounds")


def frequency_kernel(both_sides, sign_ref, x_ref, bare_ref, *refs):
    tables, out_ref = refs[:8], refs[-1]
    forth = ((tables[0][...], tables[1][...]), (tables[2][...], tables[3][...]))
    back = ((tables[4][...], tables[5][...]), (tables[6][...], tables[7][...]))
    hs = x_ref.shape[0] // 2
    tile = x_ref.shape[1:]
    lane = lax.broadcasted_iota(jnp.int32, tile, 1)
    first_half = lane < LANES // 2
    mixed = [
        [x_ref[k] + x_ref[k + hs] for k in range(hs)],
        [x_ref[k] - x_ref[k + hs] for k in range(hs)],
    ]
    for side in range(2):
        bare = bare_ref[side]
        result = []
        for parity in range(2):
            u = mixed[parity]
            pieces = []
            for k in range(0, hs, 2):
                if side == 0:
                    pieces.append(jnp.where(first_half, u[k], lane_swap(u[k + 1])))
                else:
                    pieces.append(jnp.where(first_half, lane_swap(u[k]), u[k + 1]))
            pol = product3(halves_of(jnp.concatenate(pieces, axis=1)), forth[parity], NN)
            screened = bare * bare * pol / jnp.maximum(1.0 - bare * pol, 1.0)
            if parity == 0:
                zero = lax.broadcasted_iota(jnp.int32, screened.shape, 1) == 0
                screened = jnp.where(zero, 0.5 * screened, screened)
            result.append(product3(halves_of(screened), back[parity], NN))
        for d in range(hs // 2):
            lanes = slice(LANES * d, LANES * (d + 1))
            even, odd = result[0][:, lanes], result[1][:, lanes]
            if not both_sides:
                odd = odd * sign_ref[0]
            near, far = even + odd, even - odd
            out_ref[d, side] = near
            out_ref[hs - 1 - d, side] = gathered(far, LANES - 1 - lane)
            if both_sides:
                out_ref[hs + d, side] = far
                out_ref[2 * hs - 1 - d, side] = gathered(near, LANES - 1 - lane)


def through_frequencies(x, bare, tables, block, sign, both_sides, after):
    sources, rows, _ = x.shape
    slabs = sources if both_sides else sources // 2
    return pl.pallas_call(
        lambda *refs: frequency_kernel(both_sides, *refs),
        grid=(-(-rows // block),),
        in_specs=[
            pl.BlockSpec(memory_space=pltpu.SMEM),
            pl.BlockSpec((sources, block, LANES), lambda i: (0, i, 0)),
            pl.BlockSpec((2, block, 1), lambda i: (0, i, 0)),
        ]
        + [whole(a) for a in tables]
        + [anywhere] * len(after),
        out_specs=pl.BlockSpec((slabs, 2, block, LANES), lambda i: (0, 0, i, 0)),
        out_shape=jax.ShapeDtypeStruct((slabs, 2, rows, LANES), f32),
        cost_estimate=pl.CostEstimate(
            flops=48 * rows * 512 * 512, bytes_accessed=3 * x.size * 4, transcendentals=0
        ),
        interpret=INTERPRET,
        name="through_frequencies",
    )(sign, x, bare, *tables, *after)


def line_order():
    return np.concatenate([np.arange(1, KEPT), [0]])


def back_x_table():
    table = np.zeros((2 * ROWS_X, L))
    angle = np_angle(line_order(), np.arange(L))
    table[:KEPT] = np.cos(angle) / L
    table[ROWS_X : ROWS_X + KEPT] = np.sin(angle) / L
    return table_halves(table)


def back_x_kernel(count, depth, sines, *refs):
    lower_ref, upper_ref, high_ref, low_ref, z_ref = refs
    flat = [r.reshape(r.shape[0] * r.shape[1], LANES) for r in (lower_ref, upper_ref)]
    back_x(count, depth, sines, flat, high_ref, low_ref, z_ref)


def gather_back_x_kernel(count, depth, sines, own_ref, *refs):
    blocks, (high_ref, low_ref, z_ref, flat_ref) = refs[:-4], refs[-4:]
    rows = blocks[0].shape[1]
    for k, block in enumerate(blocks):
        place = pl.ds(pl.multiple_of((own_ref[0] ^ k) * rows, 8), rows)
        for side in range(2):
            flat_ref[side, place, :] = block[side]
    back_x(count, depth, sines, [flat_ref.at[0], flat_ref.at[1]], high_ref, low_ref, z_ref)


def back_x(count, depth, sines, flat, high_ref, low_ref, z_ref):
    table = (high_ref[...], low_ref[...])
    z_ref[...] = jnp.zeros_like(z_ref)

    def lines(ky):
        rows = pl.ds(ky * HALF_L, HALF_L)
        return jnp.concatenate([flat[0][rows, :], flat[1][rows, :]], axis=0)

    def put(ky, result):
        z_ref[pl.ds(ky, KEPT, stride=depth), :] = result[:KEPT]
        z_ref[pl.ds(sines + ky, KEPT, stride=depth), :] = result[ROWS_X : ROWS_X + KEPT]

    def pair(ky):
        both = jnp.concatenate([lines(ky), lines(ky + 1)], axis=1)
        result = product3(table, halves_of(both), NN)
        put(ky, result[:, :LANES])
        put(ky + 1, result[:, LANES:])

    unrolled = 4

    def body(m, carry):
        for v in range(unrolled):
            pair(2 * (unrolled * m + v))
        return carry

    lax.fori_loop(0, count // (2 * unrolled), body, 0)
    for ky in range(count // (2 * unrolled) * 2 * unrolled, count - 1, 2):
        pair(ky)
    if count % 2:
        put(count - 1, product3(table, halves_of(lines(count - 1)), NN))


def back_x_depth(count):
    sines = -(-count // 8) * 8
    return sines, (2 * sines // 8 | 1) * 8


def back_along_x(w, count):
    sources, _, rows, _ = w.shape
    high, low = back_x_table()
    sines, depth = back_x_depth(count)
    side = lambda s: pl.BlockSpec(
        (sources, None, rows, LANES), lambda i: (0, s, 0, 0), pipeline_mode=pl.Buffered(1)
    )
    return pl.pallas_call(
        lambda *refs: back_x_kernel(count, depth, sines, *refs),
        grid=(1,),
        in_specs=[side(0), side(1), whole(high), whole(low)],
        out_specs=pl.BlockSpec((KEPT * depth, LANES), lambda i: (0, 0)),
        out_shape=jax.ShapeDtypeStruct((KEPT * depth, LANES), f32),
        cost_estimate=pl.CostEstimate(
            flops=6 * count * 256 * 256 * LANES, bytes_accessed=10 * 1024 * 1024, transcendentals=0
        ),
        compiler_params=pltpu.CompilerParams(vmem_limit_bytes=24 * MIB),
        interpret=INTERPRET,
        name="back_along_x",
    )(w, w, high, low)


def gather_back_along_x(blocks, own, count):
    _, rows, _ = blocks[0].shape
    high, low = back_x_table()
    sines, depth = back_x_depth(count)
    return pl.pallas_call(
        lambda *refs: gather_back_x_kernel(count, depth, sines, *refs),
        grid=(1,),
        in_specs=[pl.BlockSpec(memory_space=pltpu.SMEM)] + [whole(a) for a in (*blocks, high, low)],
        out_specs=pl.BlockSpec((KEPT * depth, LANES), lambda i: (0, 0)),
        out_shape=jax.ShapeDtypeStruct((KEPT * depth, LANES), f32),
        scratch_shapes=[pltpu.VMEM((2, len(blocks) * rows, LANES), f32)],
        cost_estimate=pl.CostEstimate(
            flops=6 * count * 256 * 256 * LANES, bytes_accessed=10 * 1024 * 1024, transcendentals=0
        ),
        compiler_params=pltpu.CompilerParams(vmem_limit_bytes=24 * MIB),
        interpret=INTERPRET,
        name="gather_back_along_x",
    )(own, *blocks, high, low)


def back_y_table(chunks):
    tables = []
    first = 0
    y = np.arange(LANES)
    for count in chunks:
        sines, depth = back_x_depth(count)
        ky = np.arange(first, first + count)
        angle = np_angle(ky, y)
        table = np.zeros((depth, 2 * LANES))
        table[:count, :LANES] = np_twice(ky)[:, None] * np.cos(angle)
        table[sines : sines + count, LANES:] = np_twice(ky)[:, None] * np.sin(angle)
        tables.append(table)
        first += count
    return table_halves(np.concatenate(tables, axis=0))


X_STEP = 8


def back_y_kernel(depths, *refs):
    n = len(depths)
    blocks, firsts = refs[:n], refs[n : 2 * n]
    high_ref, low_ref, own_ref, out_ref, minus_ref, plus_ref = refs[2 * n :]
    step, side = pl.program_id(0), pl.program_id(1)
    table = (high_ref[...], low_ref[...])
    lane = lax.broadcasted_iota(jnp.int32, (LANES, LANES), 1)
    turned_lane = (LANES // 2 - lane) & (LANES - 1)

    def fill(slot, parts):
        lines = jnp.concatenate(parts, axis=0).T
        result = product3(halves_of(lines), table, NN)
        cosines, sines = result[:, :LANES], result[:, LANES:]
        minus_ref[slot] = cosines - sines
        plus_ref[slot] = cosines + sines

    @pl.when((step == 0) & (side == 0))
    def _():
        fill(0, [r[...] for r in firsts])

    @pl.when(side == 0)
    def _():
        for s in range(X_STEP):
            fill(s + 1, [r[s * d : (s + 1) * d, :] for r, d in zip(blocks, depths)])

    def emit(near_ref, far_ref, slots):
        for u in range(X_STEP // 2):
            even, odd = slots[2 * u], slots[2 * u + 1]
            near = near_ref[even]
            far = gathered(far_ref[even], turned_lane)
            near_odd = lane_swap(near_ref[odd])
            far_odd = lane_swap(gathered(far_ref[odd], turned_lane))
            tiles = (
                jnp.where(lane <= HALF_L, near, far),
                jnp.where(lane < LANES // 2, far, near_odd),
                jnp.where(lane <= HALF_L - LANES // 2, near_odd, far_odd),
            )
            for i, w in enumerate(tiles):
                lanes = slice(u * PAIR + i * LANES, u * PAIR + (i + 1) * LANES)
                out_ref[:, lanes] = -own_ref[:, lanes] * w

    @pl.when(side == 0)
    def _():
        emit(minus_ref, plus_ref, list(range(X_STEP)))

    @pl.when(side == 1)
    def _():
        emit(plus_ref, minus_ref, list(range(X_STEP, 0, -1)))
        minus_ref[0] = minus_ref[X_STEP]
        plus_ref[0] = plus_ref[X_STEP]


def back_along_y(propagator, parts, chunks):
    slab, sites = propagator.shape
    high, low = back_y_table(chunks)
    depths = tuple(back_x_depth(c)[1] for c in chunks)
    width = X_STEP * L
    steps = HALF_L // X_STEP
    moving = pl.BlockSpec((slab, width), lambda i, j: (0, jnp.where(j == 0, i, 2 * steps - 1 - i)))
    return pl.pallas_call(
        lambda *refs: back_y_kernel(depths, *refs),
        grid=(steps, 2),
        in_specs=[pl.BlockSpec((X_STEP * d, LANES), lambda i, j: (i, 0)) for d in depths]
        + [pl.BlockSpec((d, LANES), lambda i, j: (HALF_L, 0)) for d in depths]
        + [whole(high), whole(low), moving],
        out_specs=moving,
        out_shape=jax.ShapeDtypeStruct((slab, sites), f32),
        scratch_shapes=[pltpu.VMEM((X_STEP + 1, LANES, LANES), f32)] * 2,
        cost_estimate=pl.CostEstimate(
            flops=6 * KEPT * 128 * 256 * 256, bytes_accessed=2 * propagator.size * 4, transcendentals=0
        ),
        compiler_params=pltpu.CompilerParams(vmem_limit_bytes=12 * MIB),
        interpret=INTERPRET,
        name="back_along_y",
    )(*parts, *parts, high, low, propagator)


CUTS = (0, 40, KEPT // 2 + 1)
CHUNKS = ((33, 12, 200, True), (32, 8, 96, False), (32, 8, 96, False))


def frequency_tables(points, slab):
    half = slab // 2
    quarter = points // 4
    slot = lax.optimization_barrier(jnp.arange(quarter, dtype=jnp.int32))
    count = lax.optimization_barrier(jnp.arange(NF // 2, dtype=jnp.int32))
    held = slot // half * slab + slot % half
    tables = []
    for times, turned in ((held, False), (slot, True)):
        for parity in (0, 1):
            n = 2 * count + parity
            a, b = (n[:, None], times[None, :]) if turned else (n[None, :], times[:, None])
            phase = a * (2 * b + 1) % (2 * points)
            table = jnp.cos(jnp.pi * phase.astype(f32) / points) * (2.0 / math.sqrt(points))
            high = lax.reduce_precision(table, 8, 7)
            tables += [high.astype(bf16), (table - high).astype(bf16)]
    return tables


def with_kernels(propagator, onsite_coupling, neighbour_strength):
    devices = lax.axis_size("tau")
    me = lax.axis_index("tau")
    slab, _ = propagator.shape
    half = slab // 2

    partner = [(d, devices - 1 - d) for d in range(devices)]
    tables = frequency_tables(slab * devices, slab)
    lines = None
    for first, last in zip(CUTS[:-1], CUTS[1:]):
        mirror = lax.ppermute(propagator[half:, first * PAIR : last * PAIR], "tau", partner)
        lines = bubble_along_y(propagator, mirror, first, last - first, lines, [] if first else tables)

    first = 0
    returned = []
    moved, turned = [], []
    sides = devices // 2
    own = (me % sides)[None].astype(jnp.int32)
    sign = jnp.where(me < sides, 1.0, -1.0)[None].astype(f32)
    for count, span, block, shared in CHUNKS:
        owners = sides if shared else devices
        rows = -(-count * HALF_L // (8 * owners)) * 8
        pol_mom = along_x([lines], first, span, rows * owners, devices // owners, moved)
        moved = [pol_mom]
        pol_mom = pol_mom.reshape(devices, rows, LANES)
        by_momentum = lax.all_to_all(pol_mom, "tau", split_axis=0, concat_axis=0, tiled=True)
        row = me % owners * rows + jnp.arange(rows, dtype=jnp.int32)
        bare = jnp.stack(
            [
                bare_potential(
                    row % HALF_L + HALF_L * side, first + row // HALF_L, onsite_coupling[0], neighbour_strength[0]
                )
                for side in (0, 1)
            ]
        )[:, :, None]
        w = through_frequencies(by_momentum, bare, tables, block, sign, not shared, turned)
        turned = [w]
        if shared:
            blocks = [lax.dynamic_index_in_dim(w, own[0] ^ k, 0, keepdims=False) for k in range(sides)]
            for k in range(1, sides):
                blocks[k] = lax.ppermute(blocks[k], "tau", [(d, d ^ k) for d in range(devices)])
            returned.append(gather_back_along_x(blocks, own, count))
        else:
            w = lax.all_to_all(w, "tau", split_axis=0, concat_axis=0, tiled=True)
            returned.append(back_along_x(w, count))
        first += count
    return back_along_y(propagator, returned, [c[0] for c in CHUNKS])


def per_device(propagator, onsite_coupling, neighbour_strength):
    slab, sites = propagator.shape
    devices = lax.axis_size("tau")
    fits = slab == LANES and sites == L * L and 4 * NF == 2 * slab * devices and devices & (devices - 1) == 0
    run = with_kernels if fits else plain
    return run(propagator, onsite_coupling, neighbour_strength)


def solution(mesh):
    in_specs = (P(("grp", "tau"), None), P("grp"), P("grp"))
    out_specs = P(("grp", "tau"), None)
    return jax.shard_map(
        per_device, mesh=mesh, in_specs=in_specs, out_specs=out_specs, check_vma=False
    )
```

time: 639 us -> 600 us (0.939)
  waiting for transfers between devices: 474 us -> 397 us
  blocking collectives: 0 us -> 41.2 us
  Pallas kernels: 117 us -> 82.3 us
  local copies, waits for them, and re-layouts: 3.68 us -> 29.3 us
  starting transfers between devices: 17.5 us -> 31 us
  other arithmetic: 24.8 us -> 16.7 us
    all_to_all x2, waiting for transfers between devices: 192 us -> 59.6 us  [with_kernels(): w = lax.all_to_all(w, 'tau', split_axis=0, concat_axis=0, tiled=True)]
    ppermute x0 -> x7, waiting for transfers between devices: none -> 81.2 us  [with_kernels(): lax.ppermute(blocks[k], 'tau', [(d, d ^ k) for d in range(devices)])]
    all_to_all x0 -> x1, blocking collectives: none -> 41.2 us  [with_kernels(): lax.all_to_all(pol_mom, 'tau', split_axis=0, concat_axis=0, tiled=True)]
    pallas_call x6 -> x12, Pallas kernels: 117 us -> 82.3 us  [the longest x3 29.6 us: through_frequencies(): pl.pallas_call(lambda *refs: frequency_kernel(both_sides, *refs), grid=(-...]
    ppermute x2, waiting for transfers between devices: 199 us -> 177 us  [with_kernels(): lax.ppermute(propagator[half:, first * PAIR:last * PAIR], 'tau', partner)]
    unnamed x0 -> x52, local copies, waits for them, and re-layouts: none -> 21 us
    ppermute x0 -> x7, starting transfers between devices: none -> 8.94 us  [with_kernels(): lax.ppermute(blocks[k], 'tau', [(d, d ^ k) for d in range(devices)])]
    all_to_all x1 -> x2, waiting for transfers between devices: 82.7 us -> 78.5 us  [with_kernels(): lax.all_to_all(pol_mom, 'tau', split_axis=0, concat_axis=0, tiled=True)]
  transfers between devices with their start and end apart: 5 -> 13, of which waited for: 5 -> 9; matrix products, arithmetic and copies ran while one was open for 4% -> 4% of each run, Pallas kernels for 3% -> 8%
where the time goes in v2:
time: 600 us; the launch traced here: 599 us
  waiting for transfers between devices  397 us (66%)
  Pallas kernels  82.3 us (14%)
  blocking collectives  41.2 us (7%)
  starting transfers between devices  31 us (5%)
  local copies, waits for them, and re-layouts  29.3 us (5%)
  other arithmetic  16.7 us (3%)
    ppermute x2, waiting for transfers between devices, with_kernels(): lax.ppermute(propagator[half:, first * PAIR:last * PAIR], 'tau', partner)  177 us
    ppermute x7, waiting for transfers between devices, with_kernels(): lax.ppermute(blocks[k], 'tau', [(d, d ^ k) for d in range(devices)])  81.2 us
    all_to_all x2, waiting for transfers between devices, with_kernels(): lax.all_to_all(pol_mom, 'tau', split_axis=0, concat_axis=0, tiled=True)  78.5 us
    all_to_all x2, waiting for transfers between devices, with_kernels(): w = lax.all_to_all(w, 'tau', split_axis=0, concat_axis=0, tiled=True)  59.6 us
    all_to_all x1, blocking collectives, with_kernels(): lax.all_to_all(pol_mom, 'tau', split_axis=0, concat_axis=0, tiled=True)  41.2 us
    pallas_call x3, Pallas kernels, through_frequencies(): pl.pallas_call(lambda *refs: frequency_kernel(both_sides, *refs), grid=(-...  29.6 us
    pallas_call x1, Pallas kernels, back_along_y(): pl.pallas_call(lambda *refs: back_y_kernel(depths, *refs), grid=(steps, 2...  22.5 us
    unnamed x52, local copies, waits for them, and re-layouts  21 us
  transfers between devices with their start and end apart: 13, of which 9 were waited for; matrix products, arithmetic and copies ran while one was open for 4% of the time, Pallas kernels for 8%

profile of v2, /device:TPU:11, one launch (start us, length us, event | category | flops | bytes accessed | tf_op | source)
XLA Modules:
  0.0 598.7 jit_solution(17790404046910086435)
XLA Ops:
  6.5 16.2 %fusion.1 = (bf16[512,512]{1,0:T(8,128)(2,1)S(1)}, bf16[512,512]{1,0:T(8,128)(2,1)S(1)}, bf16[512,512]{1,0:T(8,128)(2,1)S(1)}, bf16[512,512]{1,0:T(8,128)(2,1)S(...) fusion(s32[512]{0:T(512)S(1)} %get-tuple-element.26, ...), kind=kLoop, calls=%fused_computation.29 | loop fusion | flops 19922944 | bytes 4200448 | tf_op jit(solution)/shard_map/convert_element_type | solution.py:568
  22.8 171.4 %collective-permute-done.1.refs_1_ = f32[64,15360]{1,0:T(8,128)S(1)} collective-permute-done((f32[64,15360]{1,0:T(8,128)S(1)}, f32[64,15360]{1,0:T(8,128)S(1)}, u32[]{:S(2)}, u32[]{:S(2)}) %collective-permute-start.1) | collective-permute-done | bytes 3932192 | tf_op jit(solution)/shard_map/ppermute | solution.py:582
  194.2 6.4 %copy-done = f32[128,36864]{1,0:T(8,128)S(1)} copy-done((f32[128,36864]{1,0:T(8,128)S(1)}, f32[128,36864]{1,0:T(8,128)}, u32[]{:S(2)}) %copy-start) | copy-done | bytes 18874392
  200.6 6.6 %bubble_along_y.2.refs_5_ = f32[56,256,128]{2,1,0:T(8,128)S(1)} custom-call(f32[128,36864]{1,0:T(8,128)S(1)} %copy-done, f32[64,15360]{1,0:T(8,128)S(1)} %collective-permute-done.1.refs_1_, bf16[64,64]{1,0:T(8,128)(2,1)S(1)} %copy-done.24, bf16[256,512]{1,0:T(8,128)(2,1)S(1)} %copy-done.17, bf16[256,512]{1,0:T(8,128)(2,1)S(1)} %copy-done.16, ...), custom_call_target="tpu_custom_call" | custom-call | flops 4026531840 | bytes 11796480 | tf_op jit(solution)/shard_map/bubble_along_y/pallas_call | solution.py:204
  207.3 5.8 collective-permute-done.refs_1_
  215.8 4.5 along_x.3.refs_3_
  223.2 41.2 %all_to_all.25.refs_1_ = f32[16,192,128]{2,1,0:T(8,128)} all-to-all(f32[16,192,128]{2,1,0:T(8,128)S(1)} %bitcast.36), channel_id=1, replica_groups=mesh['grp'=2,'tau'=16] {'tau'}, dimensions={0} | all-to-all | bytes 3145728 | tf_op jit(solution)/shard_map/all_to_all | solution.py:597
  264.4 4.9 all-to-all-start
  276.1 66.0 %all-to-all-done.refs_1_ = f32[16,400,128]{2,1,0:T(8,128)} async-done(((f32[16,400,128]{2,1,0:T(8,128)}), f32[16,400,128]{2,1,0:T(8,128)}, u32[]{:S(2)}, u32[]{:S(2)}) %all-to-all-start) | async-done | bytes 3276832 | tf_op jit(solution)/shard_map/all_to_all | solution.py:597
  342.1 4.8 all-to-all-start.3
  350.3 11.1 %through_frequencies.3.refs_11_ = f32[8,2,400,128]{3,2,1,0:T(8,128)} custom-call(f32[1]{0:T(128)} %bitcast.1.refs_0_, f32[16,400,128]{2,1,0:T(8,128)} %all-to-all-done.refs_1_, f32[2,400,1]{2,1,0:T(8,128)} %copy.28.refs_2_, bf16[512,512]{1,0:T(8,128)(2,1)} %copy-done.11, bf16[512,512]{1,0:T(8,128)(2,1)} %copy-done.12, bf16[512,512]{1,0:T(8,128)(2,1)} %copy-done.9, ...), custom_call_target="tpu_custom_call" | custom-call | flops 5033164800 | bytes 9830400 | tf_op jit(solution)/shard_map/through_frequencies/pallas_call | solution.py:327
  361.4 9.2 %through_frequencies.4.refs_11_ = f32[16,2,192,128]{3,2,1,0:T(8,128)} custom-call(f32[1]{0:T(128)} %bitcast.1.refs_0_, f32[16,192,128]{2,1,0:T(8,128)} %all_to_all.25.refs_1_, f32[2,192,1]{2,1,0:T(8,128)} %copy.29.refs_2_, bf16[512,512]{1,0:T(8,128)(2,1)} %copy-done.11, bf16[512,512]{1,0:T(8,128)(2,1)} %copy-done.12, bf16[512,512]{1,0:T(8,128)(2,1)} %copy-done.9, ...), custom_call_target="tpu_custom_call" | custom-call | flops 2415919104 | bytes 4718592 | tf_op jit(solution)/shard_map/through_frequencies/pallas_call | solution.py:327
  370.6 12.5 %all-to-all-done.3.refs_1_ = f32[16,192,128]{2,1,0:T(8,128)S(1)} async-done(((f32[16,192,128]{2,1,0:T(8,128)}), f32[16,192,128]{2,1,0:T(8,128)S(1)}, u32[]{:S(2)}, u32[]{:S(2)}) %all-to-all-start.3) | async-done | bytes 1572896 | tf_op jit(solution)/shard_map/all_to_all | solution.py:597
  384.3 4.8 all-to-all-start.2
  390.1 9.3 %through_frequencies.5 = f32[16,2,192,128]{3,2,1,0:T(8,128)} custom-call(f32[1]{0:T(128)} %bitcast.1.refs_0_, f32[16,192,128]{2,1,0:T(8,128)} %copy-done.25, f32[2,192,1]{2,1,0:T(8,128)} %copy.30.refs_2_, bf16[512,512]{1,0:T(8,128)(2,1)} %copy-done.11, bf16[512,512]{1,0:T(8,128)(2,1)} %copy-done.12, bf16[512,512]{1,0:T(8,128)(2,1)} %copy-done.9, ...), custom_call_target="tpu_custom_call" | custom-call | flops 2415919104 | bytes 4718592 | tf_op jit(solution)/shard_map/through_frequencies/pallas_call | solution.py:327
  399.4 59.6 %all-to-all-done.2.refs_0_.refs_1_ = f32[16,2,192,128]{3,2,1,0:T(8,128)S(1)} async-done(((f32[16,2,192,128]{3,2,1,0:T(8,128)}), f32[16,2,192,128]{3,2,1,0:T(8,128)S(1)}, u32[]{:S(2)}, u32[]{:S(2)}) %all-to-all-start.2) | async-done | bytes 3145760 | tf_op jit(solution)/shard_map/all_to_all | solution.py:615
  459.0 4.8 all-to-all-start.4
  471.0 54.9 %collective-permute-done.8.refs_8_ = f32[2,400,128]{2,1,0:T(8,128)S(1)} collective-permute-done((f32[2,400,128]{2,1,0:T(8,128)S(1)}, f32[2,400,128]{2,1,0:T(8,128)S(1)}, u32[]{:S(2)}, u32[]{:S(2)}) %collective-permute-start.8) | collective-permute-done | bytes 409632 | tf_op jit(solution)/shard_map/ppermute | solution.py:612
  528.9 9.7 %collective-permute-done.7.refs_7_ = f32[2,400,128]{2,1,0:T(8,128)S(1)} collective-permute-done((f32[2,400,128]{2,1,0:T(8,128)S(1)}, f32[2,400,128]{2,1,0:T(8,128)S(1)}, u32[]{:S(2)}, u32[]{:S(2)}) %collective-permute-start.7) | collective-permute-done | bytes 409632 | tf_op jit(solution)/shard_map/ppermute | solution.py:612
  539.4 8.8 %collective-permute-done.6.refs_6_ = f32[2,400,128]{2,1,0:T(8,128)S(1)} collective-permute-done((f32[2,400,128]{2,1,0:T(8,128)S(1)}, f32[2,400,128]{2,1,0:T(8,128)S(1)}, u32[]{:S(2)}, u32[]{:S(2)}) %collective-permute-start.6) | collective-permute-done | bytes 409632 | tf_op jit(solution)/shard_map/ppermute | solution.py:612
  548.2 7.9 %collective-permute-done.5.refs_5_ = f32[2,400,128]{2,1,0:T(8,128)S(1)} collective-permute-done((f32[2,400,128]{2,1,0:T(8,128)S(1)}, f32[2,400,128]{2,1,0:T(8,128)S(1)}, u32[]{:S(2)}, u32[]{:S(2)}) %collective-permute-start.5) | collective-permute-done | bytes 409632 | tf_op jit(solution)/shard_map/ppermute | solution.py:612
  565.4 4.4 back_along_x.3.refs_2_.refs_5_
  569.9 6.4 %copy-done.1 = f32[128,36864]{1,0:T(8,128)S(1)} copy-done((f32[128,36864]{1,0:T(8,128)S(1)}, f32[128,36864]{1,0:T(8,128)}, u32[]{:S(2)}) %copy-start.1) | copy-done | bytes 18874392
  576.2 22.5 %back_along_y.1 = f32[128,36864]{1,0:T(8,128)} custom-call(f32[8536,128]{1,0:T(8,128)S(1)} %copy-done.5, f32[6984,128]{1,0:T(8,128)S(1)} %copy-done.7, f32[6984,128]{1,0:T(8,128)S(1)} %back_along_x.3.refs_2_.refs_5_, f32[8536,128]{1,0:T(8,128)S(1)} %copy-done.5, f32[6984,128]{1,0:T(8,128)S(1)} %copy-done.7, f32[6984,128]{1,0:T(8,128)S(1)} %back_along_x.3.refs_2_.refs_5_, ...), custom_call_target="tpu_custom_call" | custom-call | flops 4882169856 | bytes 37748736 | tf_op jit(solution)/shard_map/back_along_y/pallas_call | solution.py:532
  (82 shorter events, 43.5 us)
Async XLA Ops:
  2.4 191.8 %copy-start.16 = (bf16[256,512]{1,0:T(8,128)(2,1)S(1)}, bf16[256,512]{1,0:T(8,128)(2,1)}, u32[]{:S(2)}) copy-start(bf16[256,512]{1,0:T(8,128)(2,1)} %constant.245.clone.refs_4_) | copy-start | bytes 786436
  2.4 191.8 %copy-start.17 = (bf16[256,512]{1,0:T(8,128)(2,1)S(1)}, bf16[256,512]{1,0:T(8,128)(2,1)}, u32[]{:S(2)}) copy-start(bf16[256,512]{1,0:T(8,128)(2,1)} %constant.244.clone.refs_3_) | copy-start | bytes 786436
  2.4 191.8 %copy-start.24 = (bf16[64,64]{1,0:T(8,128)(2,1)S(1)}, bf16[64,64]{1,0:T(8,128)(2,1)}, u32[]{:S(2)}) copy-start(bf16[64,64]{1,0:T(8,128)(2,1)} %constant.246.clone.refs_2_) | copy-start | bytes 24580
  2.4 191.7 %collective-permute-start.1 = (f32[64,15360]{1,0:T(8,128)S(1)}, f32[64,15360]{1,0:T(8,128)S(1)}, u32[]{:S(2)}, u32[]{:S(2)}) collective-permute-start(f32[64,15360]{1,0:T(8,128)S(1)} %slice.7), channel_id=1, source_target_pairs={{0,15},{1,14},{2,13},{3,12},{4,11},{5,10},{6,9},{7,8},{8,7},{9,6},... | collective-permute-start | bytes 11796488 | tf_op jit(solution)/shard_map/ppermute | solution.py:582
  5.6 207.5 %collective-permute-start = (f32[64,3456]{1,0:T(8,128)S(1)}, f32[64,3456]{1,0:T(8,128)S(1)}, u32[]{:S(2)}, u32[]{:S(2)}) collective-permute-start(f32[64,3456]{1,0:T(8,128)S(1)} %slice.6), channel_id=1, source_target_pairs={{0,15},{1,14},{2,13},{3,12},{4,11},{5,10},{6,9},{7,8},{8,7},{9,6},... | collective-permute-start | bytes 2654216 | tf_op jit(solution)/shard_map/ppermute | solution.py:582
  22.7 184.5 %copy-start.8 = (bf16[512,512]{1,0:T(8,128)(2,1)}, bf16[512,512]{1,0:T(8,128)(2,1)S(1)}, u32[]{:S(2)}) copy-start(bf16[512,512]{1,0:T(8,128)(2,1)S(1)} %get-tuple-element.15.refs_8_.refs_6_) | copy-start | bytes 1572868
  22.7 184.5 %copy-start.9 = (bf16[512,512]{1,0:T(8,128)(2,1)}, bf16[512,512]{1,0:T(8,128)(2,1)S(1)}, u32[]{:S(2)}) copy-start(bf16[512,512]{1,0:T(8,128)(2,1)S(1)} %get-tuple-element.16.refs_7_.refs_5_) | copy-start | bytes 1572868
  22.7 184.5 %copy-start.10 = (bf16[512,512]{1,0:T(8,128)(2,1)}, bf16[512,512]{1,0:T(8,128)(2,1)S(1)}, u32[]{:S(2)}) copy-start(bf16[512,512]{1,0:T(8,128)(2,1)S(1)} %get-tuple-element.19.refs_12_.refs_10_) | copy-start | bytes 1572868
  22.7 184.5 %copy-start.11 = (bf16[512,512]{1,0:T(8,128)(2,1)}, bf16[512,512]{1,0:T(8,128)(2,1)S(1)}, u32[]{:S(2)}) copy-start(bf16[512,512]{1,0:T(8,128)(2,1)S(1)} %get-tuple-element.20.refs_5_.refs_3_) | copy-start | bytes 1572868
  22.7 184.5 %copy-start.12 = (bf16[512,512]{1,0:T(8,128)(2,1)}, bf16[512,512]{1,0:T(8,128)(2,1)S(1)}, u32[]{:S(2)}) copy-start(bf16[512,512]{1,0:T(8,128)(2,1)S(1)} %get-tuple-element.21.refs_6_.refs_4_) | copy-start | bytes 1572868
  22.7 184.5 %copy-start.13 = (bf16[512,512]{1,0:T(8,128)(2,1)}, bf16[512,512]{1,0:T(8,128)(2,1)S(1)}, u32[]{:S(2)}) copy-start(bf16[512,512]{1,0:T(8,128)(2,1)S(1)} %get-tuple-element.22.refs_9_.refs_7_) | copy-start | bytes 1572868
  22.8 184.5 %copy-start.14 = (bf16[512,512]{1,0:T(8,128)(2,1)}, bf16[512,512]{1,0:T(8,128)(2,1)S(1)}, u32[]{:S(2)}) copy-start(bf16[512,512]{1,0:T(8,128)(2,1)S(1)} %get-tuple-element.23.refs_10_.refs_8_) | copy-start | bytes 1572868
  22.8 184.5 %copy-start.15 = (bf16[512,512]{1,0:T(8,128)(2,1)}, bf16[512,512]{1,0:T(8,128)(2,1)S(1)}, u32[]{:S(2)}) copy-start(bf16[512,512]{1,0:T(8,128)(2,1)S(1)} %get-tuple-element.24.refs_11_.refs_9_) | copy-start | bytes 1572868
  264.4 77.8 %all-to-all-start = ((f32[16,400,128]{2,1,0:T(8,128)}), f32[16,400,128]{2,1,0:T(8,128)}, u32[]{:S(2)}, u32[]{:S(2)}) async-start(f32[16,400,128]{2,1,0:T(8,128)} %bitcast.3), calls=%async_computation | async-start | bytes 6553600 | tf_op jit(solution)/shard_map/all_to_all | solution.py:597
  342.1 41.0 %all-to-all-start.3 = ((f32[16,192,128]{2,1,0:T(8,128)}), f32[16,192,128]{2,1,0:T(8,128)S(1)}, u32[]{:S(2)}, u32[]{:S(2)}) async-start(f32[16,192,128]{2,1,0:T(8,128)} %bitcast.17), calls=%async_computation.3 | async-start | bytes 3145728 | tf_op jit(solution)/shard_map/all_to_all | solution.py:597
  384.3 74.7 %all-to-all-start.2 = ((f32[16,2,192,128]{3,2,1,0:T(8,128)}), f32[16,2,192,128]{3,2,1,0:T(8,128)S(1)}, u32[]{:S(2)}, u32[]{:S(2)}) async-start(f32[16,2,192,128]{3,2,1,0:T(8,128)} %through_frequencies.4.refs_11_), calls=%async_computation.2 | async-start | bytes 6291456 | tf_op jit(solution)/shard_map/all_to_all | solution.py:615
  459.0 106.4 %all-to-all-start.4 = ((f32[16,2,192,128]{3,2,1,0:T(8,128)}), f32[16,2,192,128]{3,2,1,0:T(8,128)}, u32[]{:S(2)}, u32[]{:S(2)}) async-start(f32[16,2,192,128]{3,2,1,0:T(8,128)} %through_frequencies.5), calls=%async_computation.4 | async-start | bytes 6291456 | tf_op jit(solution)/shard_map/all_to_all | solution.py:615
  465.9 59.9 %collective-permute-start.8 = (f32[2,400,128]{2,1,0:T(8,128)S(1)}, f32[2,400,128]{2,1,0:T(8,128)S(1)}, u32[]{:S(2)}, u32[]{:S(2)}) collective-permute-start(f32[2,400,128]{2,1,0:T(8,128)S(1)} %get-tuple-element.5), channel_id=1, source_target_pairs={{0,7},{1,6},{2,5},{3,4},{4,3},{5,2},{6,1},{7,0},{8,15},{9,14},{10,... | collective-permute-start | bytes 1228808 | tf_op jit(solution)/shard_map/ppermute | solution.py:612
  466.2 72.3 %collective-permute-start.7 = (f32[2,400,128]{2,1,0:T(8,128)S(1)}, f32[2,400,128]{2,1,0:T(8,128)S(1)}, u32[]{:S(2)}, u32[]{:S(2)}) collective-permute-start(f32[2,400,128]{2,1,0:T(8,128)S(1)} %get-tuple-element.6), channel_id=1, source_target_pairs={{0,6},{1,7},{2,4},{3,5},{4,2},{5,3},{6,0},{7,1},{8,14},{9,15},{10,... | collective-permute-start | bytes 1228808 | tf_op jit(solution)/shard_map/ppermute | solution.py:612
  468.6 79.5 %collective-permute-start.6 = (f32[2,400,128]{2,1,0:T(8,128)S(1)}, f32[2,400,128]{2,1,0:T(8,128)S(1)}, u32[]{:S(2)}, u32[]{:S(2)}) collective-permute-start(f32[2,400,128]{2,1,0:T(8,128)S(1)} %get-tuple-element.7), channel_id=1, source_target_pairs={{0,5},{1,4},{2,7},{3,6},{4,1},{5,0},{6,3},{7,2},{8,13},{9,12},{10,... | collective-permute-start | bytes 1228808 | tf_op jit(solution)/shard_map/ppermute | solution.py:612
  469.2 86.9 %collective-permute-start.5 = (f32[2,400,128]{2,1,0:T(8,128)S(1)}, f32[2,400,128]{2,1,0:T(8,128)S(1)}, u32[]{:S(2)}, u32[]{:S(2)}) collective-permute-start(f32[2,400,128]{2,1,0:T(8,128)S(1)} %get-tuple-element.8), channel_id=1, source_target_pairs={{0,4},{1,5},{2,6},{3,7},{4,0},{5,1},{6,2},{7,3},{8,12},{9,13},{10,... | collective-permute-start | bytes 1228808 | tf_op jit(solution)/shard_map/ppermute | solution.py:612
  470.4 85.7 %collective-permute-start.4 = (f32[2,400,128]{2,1,0:T(8,128)S(1)}, f32[2,400,128]{2,1,0:T(8,128)S(1)}, u32[]{:S(2)}, u32[]{:S(2)}) collective-permute-start(f32[2,400,128]{2,1,0:T(8,128)S(1)} %get-tuple-element.9), channel_id=1, source_target_pairs={{0,3},{1,2},{2,1},{3,0},{4,7},{5,6},{6,5},{7,4},{8,11},{9,10},{10,... | collective-permute-start | bytes 1228808 | tf_op jit(solution)/shard_map/ppermute | solution.py:612
  525.8 30.3 %collective-permute-start.3 = (f32[2,400,128]{2,1,0:T(8,128)S(1)}, f32[2,400,128]{2,1,0:T(8,128)S(1)}, u32[]{:S(2)}, u32[]{:S(2)}) collective-permute-start(f32[2,400,128]{2,1,0:T(8,128)S(1)} %get-tuple-element.10), channel_id=1, source_target_pairs={{0,2},{1,3},{2,0},{3,1},{4,6},{5,7},{6,4},{7,5},{8,10},{9,11},{10,... | collective-permute-start | bytes 1228808 | tf_op jit(solution)/shard_map/ppermute | solution.py:612
  538.5 17.6 %collective-permute-start.2 = (f32[2,400,128]{2,1,0:T(8,128)S(1)}, f32[2,400,128]{2,1,0:T(8,128)S(1)}, u32[]{:S(2)}, u32[]{:S(2)}) collective-permute-start(f32[2,400,128]{2,1,0:T(8,128)S(1)} %get-tuple-element.11), channel_id=1, source_target_pairs={{0,1},{1,0},{2,3},{3,2},{4,5},{5,4},{6,7},{7,6},{8,9},{9,8},{10,11... | collective-permute-start | bytes 1228808 | tf_op jit(solution)/shard_map/ppermute | solution.py:612
  (15 other events, 244.9 us)

commit v3 on v2

--- a/solution.py
+++ b/solution.py
@@ -362,8 +362,8 @@
     back_x(count, depth, sines, flat, high_ref, low_ref, z_ref)
 
 
-def gather_back_x_kernel(count, depth, sines, own_ref, *refs):
-    blocks, (high_ref, low_ref, z_ref, flat_ref) = refs[:-4], refs[-4:]
+def gather_back_x_kernel(sources, count, depth, sines, own_ref, *refs):
+    blocks, (high_ref, low_ref), (z_ref, flat_ref) = refs[:sources], refs[sources : sources + 2], refs[-2:]
     rows = blocks[0].shape[1]
     for k, block in enumerate(blocks):
         place = pl.ds(pl.multiple_of((own_ref[0] ^ k) * rows, 8), rows)
@@ -431,14 +431,15 @@
     )(w, w, high, low)
 
 
-def gather_back_along_x(blocks, own, count):
+def gather_back_along_x(blocks, own, count, after):
     _, rows, _ = blocks[0].shape
     high, low = back_x_table()
     sines, depth = back_x_depth(count)
     return pl.pallas_call(
-        lambda *refs: gather_back_x_kernel(count, depth, sines, *refs),
+        lambda *refs: gather_back_x_kernel(len(blocks), count, depth, sines, *refs),
         grid=(1,),
-        in_specs=[pl.BlockSpec(memory_space=pltpu.SMEM)] + [whole(a) for a in (*blocks, high, low)],
+        in_specs=[pl.BlockSpec(memory_space=pltpu.SMEM)] + [whole(a) for a in (*blocks, high, low)]
+        + [anywhere] * len(after),
         out_specs=pl.BlockSpec((KEPT * depth, LANES), lambda i: (0, 0)),
         out_shape=jax.ShapeDtypeStruct((KEPT * depth, LANES), f32),
         scratch_shapes=[pltpu.VMEM((2, len(blocks) * rows, LANES), f32)],
@@ -448,12 +449,11 @@
         compiler_params=pltpu.CompilerParams(vmem_limit_bytes=24 * MIB),
         interpret=INTERPRET,
         name="gather_back_along_x",
-    )(own, *blocks, high, low)
-
-
-def back_y_table(chunks):
+    )(own, *blocks, high, low, *after)
+
+
+def back_y_table(first, chunks):
     tables = []
-    first = 0
     y = np.arange(LANES)
     for count in chunks:
         sines, depth = back_x_depth(count)
@@ -467,35 +467,70 @@
     return table_halves(np.concatenate(tables, axis=0))
 
 
-X_STEP = 8
-
-
-def back_y_kernel(depths, *refs):
-    n = len(depths)
-    blocks, firsts = refs[:n], refs[n : 2 * n]
-    high_ref, low_ref, own_ref, out_ref, minus_ref, plus_ref = refs[2 * n :]
+X_STEP = 32
+
+
+def turned_lines(parts, table):
+    result = product3(halves_of(jnp.concatenate(parts, axis=0).T), table, NN)
+    cosines, sines = result[:, :LANES], result[:, LANES:]
+    return cosines - sines, cosines + sines
+
+
+def partial_back_y_kernel(depths, *refs):
+    blocks, (high_ref, low_ref, minus_ref, plus_ref) = refs[:-4], refs[-4:]
+    table = (high_ref[...], low_ref[...])
+    for s in range(minus_ref.shape[0]):
+        lines = [r[s * d : (s + 1) * d, :] for r, d in zip(blocks, depths)]
+        minus_ref[s], plus_ref[s] = turned_lines(lines, table)
+
+
+def partial_back_along_y(parts, chunks):
+    high, low = back_y_table(0, chunks)
+    depths = tuple(back_x_depth(c)[1] for c in chunks)
+    step = 8
+    line = jax.ShapeDtypeStruct((KEPT, LANES, LANES), f32)
+    return pl.pallas_call(
+        lambda *refs: partial_back_y_kernel(depths, *refs),
+        grid=(-(-KEPT // step),),
+        in_specs=[pl.BlockSpec((step * d, LANES), lambda i: (i, 0)) for d in depths] + [whole(high), whole(low)],
+        out_specs=[pl.BlockSpec((step, LANES, LANES), lambda i: (i, 0, 0))] * 2,
+        out_shape=[line, line],
+        cost_estimate=pl.CostEstimate(
+            flops=6 * KEPT * 128 * 256 * 256, bytes_accessed=24 * MIB, transcendentals=0
+        ),
+        interpret=INTERPRET,
+        name="partial_back_along_y",
+    )(*parts, high, low)
+
+
+def back_y_kernel(depth, *refs):
+    halves, heads, zeroth = refs[:3], refs[3:6], refs[6:9]
+    high_ref, low_ref, own_ref, out_ref, minus_ref, plus_ref = refs[9:]
     step, side = pl.program_id(0), pl.program_id(1)
     table = (high_ref[...], low_ref[...])
     lane = lax.broadcasted_iota(jnp.int32, (LANES, LANES), 1)
     turned_lane = (LANES // 2 - lane) & (LANES - 1)
-
-    def fill(slot, parts):
-        lines = jnp.concatenate(parts, axis=0).T
-        result = product3(halves_of(lines), table, NN)
-        cosines, sines = result[:, :LANES], result[:, LANES:]
-        minus_ref[slot] = cosines - sines
-        plus_ref[slot] = cosines + sines
+    ring = 2 * X_STEP
+
+    def fill(source, s, line):
+        z_ref, early_minus_ref, early_plus_ref = source
+        minus, plus = turned_lines([z_ref[s * depth : (s + 1) * depth, :]], table)
+        slot = line & (ring - 1)
+        minus_ref[slot] = minus + early_minus_ref[s]
+        plus_ref[slot] = plus + early_plus_ref[s]
 
     @pl.when((step == 0) & (side == 0))
     def _():
-        fill(0, [r[...] for r in firsts])
-
-    @pl.when(side == 0)
-    def _():
-        for s in range(X_STEP):
-            fill(s + 1, [r[s * d : (s + 1) * d, :] for r, d in zip(blocks, depths)])
-
-    def emit(near_ref, far_ref, slots):
+        fill(zeroth, 0, step)
+        for s in range(X_STEP // 2):
+            fill(heads, s, step + 1 + s)
+
+    half = jnp.minimum(2 * step + 1 + side, 2 * HALF_L // X_STEP - 1)
+    for s in range(X_STEP // 2):
+        fill(halves, s, half * (X_STEP // 2) + 1 + s)
+
+    def emit(near_ref, far_ref, offsets):
+        slots = [(step * X_STEP + s) & (ring - 1) for s in offsets]
         for u in range(X_STEP // 2):
             even, odd = slots[2 * u], slots[2 * u + 1]
             near = near_ref[even]
@@ -513,42 +548,79 @@
 
     @pl.when(side == 0)
     def _():
-        emit(minus_ref, plus_ref, list(range(X_STEP)))
+        emit(minus_ref, plus_ref, range(X_STEP))
 
     @pl.when(side == 1)
     def _():
-        emit(plus_ref, minus_ref, list(range(X_STEP, 0, -1)))
-        minus_ref[0] = minus_ref[X_STEP]
-        plus_ref[0] = plus_ref[X_STEP]
-
-
-def back_along_y(propagator, parts, chunks):
+        emit(plus_ref, minus_ref, range(X_STEP, 0, -1))
+
+
+def back_along_y(propagator, early, last, first, count):
     slab, sites = propagator.shape
-    high, low = back_y_table(chunks)
-    depths = tuple(back_x_depth(c)[1] for c in chunks)
+    high, low = back_y_table(first, [count])
+    depth = back_x_depth(count)[1]
     width = X_STEP * L
     steps = HALF_L // X_STEP
+    half = X_STEP // 2
     moving = pl.BlockSpec((slab, width), lambda i, j: (0, jnp.where(j == 0, i, 2 * steps - 1 - i)))
+
+    def lines(size, index):
+        return [pl.BlockSpec((size * depth, LANES), lambda i, j: (index(i, j), 0))] + [
+            pl.BlockSpec((size, LANES, LANES), lambda i, j: (index(i, j), 0, 0))
+        ] * 2
+
+    sources = (last, *early)
     return pl.pallas_call(
-        lambda *refs: back_y_kernel(depths, *refs),
+        lambda *refs: back_y_kernel(depth, *refs),
         grid=(steps, 2),
-        in_specs=[pl.BlockSpec((X_STEP * d, LANES), lambda i, j: (i, 0)) for d in depths]
-        + [pl.BlockSpec((d, LANES), lambda i, j: (HALF_L, 0)) for d in depths]
+        in_specs=lines(half, lambda i, j: jnp.minimum(2 * i + 1 + j, 2 * steps - 1))
+        + lines(half, lambda i, j: 0)
+        + lines(1, lambda i, j: HALF_L)
         + [whole(high), whole(low), moving],
         out_specs=moving,
         out_shape=jax.ShapeDtypeStruct((slab, sites), f32),
-        scratch_shapes=[pltpu.VMEM((X_STEP + 1, LANES, LANES), f32)] * 2,
+        scratch_shapes=[pltpu.VMEM((2 * X_STEP, LANES, LANES), f32)] * 2,
         cost_estimate=pl.CostEstimate(
             flops=6 * KEPT * 128 * 256 * 256, bytes_accessed=2 * propagator.size * 4, transcendentals=0
         ),
-        compiler_params=pltpu.CompilerParams(vmem_limit_bytes=12 * MIB),
         interpret=INTERPRET,
         name="back_along_y",
-    )(*parts, *parts, high, low, propagator)
+    )(*sources, *sources, *sources, high, low, propagator)
 
 
 CUTS = (0, 40, KEPT // 2 + 1)
-CHUNKS = ((33, 12, 200, True), (32, 8, 96, False), (32, 8, 96, False))
+CHUNKS = ((32, 8, 96, False), (33, 12, 200, True), (32, 8, 96, False))
+
+
+def token(x):
+    return lax.slice(x.reshape(-1, LANES), (0, 0), (8, LANES))
+
+
+def chunk_firsts():
+    return [sum(c[0] for c in CHUNKS[:i]) for i in range(len(CHUNKS))]
+
+
+def pick_kernel(own_ref, w_ref, *refs):
+    slabs = w_ref.shape[0]
+    for k, out_ref in enumerate(refs[-slabs:]):
+        out_ref[...] = w_ref[own_ref[0] ^ k]
+
+
+def picked(w, own, after):
+    shape = w.shape[1:]
+    return list(
+        pl.pallas_call(
+            pick_kernel,
+            grid=(1,),
+            in_specs=[pl.BlockSpec(memory_space=pltpu.SMEM), whole(w)] + [anywhere] * len(after),
+            out_specs=[pl.BlockSpec(shape, lambda i: (0, 0, 0))] * w.shape[0],
+            out_shape=[jax.ShapeDtypeStruct(shape, f32)] * w.shape[0],
+            cost_estimate=pl.CostEstimate(flops=0, bytes_accessed=8 * w.size, transcendentals=0),
+            compiler_params=pltpu.CompilerParams(vmem_limit_bytes=16 * MIB),
+            interpret=INTERPRET,
+            name="picked",
+        )(own, w, *after)
+    )
 
 
 def frequency_tables(points, slab):
@@ -582,17 +654,16 @@
         mirror = lax.ppermute(propagator[half:, first * PAIR : last * PAIR], "tau", partner)
         lines = bubble_along_y(propagator, mirror, first, last - first, lines, [] if first else tables)
 
-    first = 0
-    returned = []
-    moved, turned = [], []
     sides = devices // 2
     own = (me % sides)[None].astype(jnp.int32)
     sign = jnp.where(me < sides, 1.0, -1.0)[None].astype(f32)
-    for count, span, block, shared in CHUNKS:
+    firsts = chunk_firsts()
+    moved, turned = [], []
+    for i, (first, (count, span, block, shared)) in enumerate(zip(firsts, CHUNKS)):
         owners = sides if shared else devices
         rows = -(-count * HALF_L // (8 * owners)) * 8
-        pol_mom = along_x([lines], first, span, rows * owners, devices // owners, moved)
-        moved = [pol_mom]
+        pol_mom = along_x([lines], first, span, rows * owners, devices // owners, [token(m) for m in moved[-1:]] + [token(w) for w in turned[: max(i - 1, 0)]])
+        moved.append(pol_mom)
         pol_mom = pol_mom.reshape(devices, rows, LANES)
         by_momentum = lax.all_to_all(pol_mom, "tau", split_axis=0, concat_axis=0, tiled=True)
         row = me % owners * rows + jnp.arange(rows, dtype=jnp.int32)
@@ -604,18 +675,28 @@
                 for side in (0, 1)
             ]
         )[:, :, None]
-        w = through_frequencies(by_momentum, bare, tables, block, sign, not shared, turned)
-        turned = [w]
+        turned.append(through_frequencies(by_momentum, bare, tables, block, sign, not shared, [token(w) for w in turned[-1:]]))
+
+    def exchanged(blocks):
+        for k in range(1, len(blocks)):
+            blocks[k] = lax.ppermute(blocks[k], "tau", [(d, d ^ k) for d in range(devices)])
+        return blocks
+
+    returned = []
+    counts = [c[0] for c in CHUNKS]
+    for first, (count, _, _, shared), w in zip(firsts, CHUNKS, turned):
         if shared:
-            blocks = [lax.dynamic_index_in_dim(w, own[0] ^ k, 0, keepdims=False) for k in range(sides)]
-            for k in range(1, sides):
-                blocks[k] = lax.ppermute(blocks[k], "tau", [(d, d ^ k) for d in range(devices)])
-            returned.append(gather_back_along_x(blocks, own, count))
+            blocks = exchanged(picked(w, own, []))
+            returned.append(gather_back_along_x(blocks, own, count, []))
+        elif w is turned[-1]:
+            place = me[None].astype(jnp.int32)
+            blocks = exchanged(picked(w, place, []))
+            early = partial_back_along_y(returned, counts[:-1])
+            last = gather_back_along_x(blocks, place, count, [token(e) for e in early])
         else:
             w = lax.all_to_all(w, "tau", split_axis=0, concat_axis=0, tiled=True)
             returned.append(back_along_x(w, count))
-        first += count
-    return back_along_y(propagator, returned, [c[0] for c in CHUNKS])
+    return back_along_y(propagator, early, last, firsts[-1], counts[-1])
 
 
 def per_device(propagator, onsite_coupling, neighbour_strength):

time: 600 us -> 604 us (level)
  waiting for transfers between devices: 397 us -> 271 us
  blocking collectives: 41.2 us -> 118 us
  Pallas kernels: 82.3 us -> 103 us
  starting transfers between devices: 31 us -> 48.8 us
  local copies, waits for them, and re-layouts: 29.3 us -> 41.1 us
    all_to_all x1 -> x2, blocking collectives: 41.2 us -> 118 us  [with_kernels(): lax.all_to_all(pol_mom, 'tau', split_axis=0, concat_axis=0, tiled=True)]
    all_to_all x2 -> x1, waiting for transfers between devices: 59.6 us -> 0.01 us  [with_kernels(): w = lax.all_to_all(w, 'tau', split_axis=0, concat_axis=0, tiled=True)]
    all_to_all x2 -> x1, waiting for transfers between devices: 78.5 us -> 26.9 us  [with_kernels(): lax.all_to_all(pol_mom, 'tau', split_axis=0, concat_axis=0, tiled=True)]
    ppermute x7 -> x22, starting transfers between devices: 8.94 us -> 35.3 us  [exchanged(): lax.ppermute(blocks[k], 'tau', [(d, d ^ k) for d in range(devices)])]
    pallas_call x2 -> x6, Pallas kernels: 25.4 us -> 51.4 us  [the longest x1 26.1 us: back_along_y(): pl.pallas_call(lambda *refs: back_y_kernel(depth, *refs), grid=(steps, 2)...]
    ppermute x7 -> x22, waiting for transfers between devices: 81.2 us -> 67 us  [exchanged(): lax.ppermute(blocks[k], 'tau', [(d, d ^ k) for d in range(devices)])]
    unnamed x52 -> x84, local copies, waits for them, and re-layouts: 21 us -> 30.9 us
  transfers between devices with their start and end apart: 13 -> 26, of which waited for: 9 -> 16; matrix products, arithmetic and copies ran while one was open for 4% -> 4% of each run, Pallas kernels for 8% -> 9%
where the time goes in v3:
time: 604 us; the launch traced here: 601 us
  waiting for transfers between devices  271 us (45%)
  blocking collectives  118 us (20%)
  Pallas kernels  103 us (17%)
  starting transfers between devices  48.8 us (8%)
  local copies, waits for them, and re-layouts  41.1 us (7%)
  other arithmetic  16.7 us (3%)
    ppermute x2, waiting for transfers between devices, with_kernels(): lax.ppermute(propagator[half:, first * PAIR:last * PAIR], 'tau', partner)  177 us
    all_to_all x2, blocking collectives, with_kernels(): lax.all_to_all(pol_mom, 'tau', split_axis=0, concat_axis=0, tiled=True)  118 us
    ppermute x22, waiting for transfers between devices, exchanged(): lax.ppermute(blocks[k], 'tau', [(d, d ^ k) for d in range(devices)])  67 us
    ppermute x22, starting transfers between devices, exchanged(): lax.ppermute(blocks[k], 'tau', [(d, d ^ k) for d in range(devices)])  35.3 us
    unnamed x84, local copies, waits for them, and re-layouts  30.9 us
    pallas_call x3, Pallas kernels, through_frequencies(): pl.pallas_call(lambda *refs: frequency_kernel(both_sides, *refs), grid=(-...  29.6 us
    all_to_all x1, waiting for transfers between devices, with_kernels(): lax.all_to_all(pol_mom, 'tau', split_axis=0, concat_axis=0, tiled=True)  26.9 us
    pallas_call x1, Pallas kernels, back_along_y(): pl.pallas_call(lambda *refs: back_y_kernel(depth, *refs), grid=(steps, 2)...  26.1 us
  transfers between devices with their start and end apart: 26, of which 16 were waited for; matrix products, arithmetic and copies ran while one was open for 4% of the time, Pallas kernels for 9%

profile of v3, /device:TPU:11, one launch (start us, length us, event | category | flops | bytes accessed | tf_op | source)
XLA Modules:
  0.0 600.9 jit_solution(7033321024698019434)
XLA Ops:
  6.5 16.2 %fusion.1 = (bf16[512,512]{1,0:T(8,128)(2,1)S(1)}, bf16[512,512]{1,0:T(8,128)(2,1)S(1)}, bf16[512,512]{1,0:T(8,128)(2,1)S(1)}, bf16[512,512]{1,0:T(8,128)(2,1)S(...) fusion(s32[512]{0:T(512)S(1)} %get-tuple-element.70, ...), kind=kLoop, calls=%fused_computation.29 | loop fusion | flops 19922944 | bytes 4200448 | tf_op jit(solution)/shard_map/convert_element_type | solution.py:640
  22.8 171.4 %collective-permute-done.1.refs_1_ = f32[64,15360]{1,0:T(8,128)S(1)} collective-permute-done((f32[64,15360]{1,0:T(8,128)S(1)}, f32[64,15360]{1,0:T(8,128)S(1)}, u32[]{:S(2)}, u32[]{:S(2)}) %collective-permute-start.1) | collective-permute-done | bytes 3932192 | tf_op jit(solution)/shard_map/ppermute | solution.py:654
  194.2 6.4 %copy-done = f32[128,36864]{1,0:T(8,128)S(1)} copy-done((f32[128,36864]{1,0:T(8,128)S(1)}, f32[128,36864]{1,0:T(8,128)}, u32[]{:S(2)}) %copy-start) | copy-done | bytes 18874392
  200.6 6.6 %bubble_along_y.2.refs_5_ = f32[56,256,128]{2,1,0:T(8,128)S(1)} custom-call(f32[128,36864]{1,0:T(8,128)S(1)} %copy-done, f32[64,15360]{1,0:T(8,128)S(1)} %collective-permute-done.1.refs_1_, bf16[64,64]{1,0:T(8,128)(2,1)S(1)} %copy-done.35, bf16[256,512]{1,0:T(8,128)(2,1)S(1)} %copy-done.18, bf16[256,512]{1,0:T(8,128)(2,1)S(1)} %copy-done.17, ...), custom_call_target="tpu_custom_call" | custom-call | flops 4026531840 | bytes 11796480 | tf_op jit(solution)/shard_map/bubble_along_y/pallas_call | solution.py:204
  207.3 5.8 collective-permute-done.refs_1_
  215.8 4.2 along_x.3
  220.1 5.2 all-to-all-start
  234.7 26.9 %all-to-all-done.refs_1_ = f32[16,192,128]{2,1,0:T(8,128)} async-done(((f32[16,192,128]{2,1,0:T(8,128)}), f32[16,192,128]{2,1,0:T(8,128)}, u32[]{:S(2)}, u32[]{:S(2)}) %all-to-all-start) | async-done | bytes 1572896 | tf_op jit(solution)/shard_map/all_to_all | solution.py:668
  261.6 9.3 %through_frequencies.3 = f32[16,2,192,128]{3,2,1,0:T(8,128)} custom-call(f32[1]{0:T(128)} %bitcast.1.refs_0_, f32[16,192,128]{2,1,0:T(8,128)} %all-to-all-done.refs_1_, f32[2,192,1]{2,1,0:T(8,128)} %copy.30.refs_2_, bf16[512,512]{1,0:T(8,128)(2,1)} %copy-done.9, bf16[512,512]{1,0:T(8,128)(2,1)} %copy-done.10, bf16[512,512]{1,0:T(8,128)(2,1)} %copy-done.7, ...), custom_call_target="tpu_custom_call" | custom-call | flops 2415919104 | bytes 4718592 | tf_op jit(solution)/shard_map/through_frequencies/pallas_call | solution.py:327
  277.6 40.7 %all_to_all.20.refs_1_ = f32[16,192,128]{2,1,0:T(8,128)} all-to-all(f32[16,192,128]{2,1,0:T(8,128)S(1)} %bitcast.30), channel_id=1, replica_groups=mesh['grp'=2,'tau'=16] {'tau'}, dimensions={0} | all-to-all | bytes 3145728 | tf_op jit(solution)/shard_map/all_to_all | solution.py:668
  318.3 77.4 %all_to_all.21.refs_1_ = f32[16,400,128]{2,1,0:T(8,128)} all-to-all(f32[16,400,128]{2,1,0:T(8,128)S(1)} %bitcast.29), channel_id=1, replica_groups=mesh['grp'=2,'tau'=16] {'tau'}, dimensions={0} | all-to-all | bytes 6553600 | tf_op jit(solution)/shard_map/all_to_all | solution.py:668
  395.7 5.6 all-to-all-start.3
  403.4 11.1 %through_frequencies.4.w_ref = f32[8,2,400,128]{3,2,1,0:T(8,128)} custom-call(f32[1]{0:T(128)} %bitcast.1.refs_0_, f32[16,400,128]{2,1,0:T(8,128)} %all_to_all.21.refs_1_, f32[2,400,1]{2,1,0:T(8,128)} %copy.31.refs_2_, bf16[512,512]{1,0:T(8,128)(2,1)} %copy-done.9, bf16[512,512]{1,0:T(8,128)(2,1)} %copy-done.10, bf16[512,512]{1,0:T(8,128)(2,1)} %copy-done.7, ...), custom_call_target="tpu_custom_call" | custom-call | flops 5033164800 | bytes 9830400 | tf_op jit(solution)/shard_map/through_frequencies/pallas_call | solution.py:327
  424.0 9.2 %through_frequencies.5.w_ref = f32[16,2,192,128]{3,2,1,0:T(8,128)} custom-call(f32[1]{0:T(128)} %bitcast.1.refs_0_, f32[16,192,128]{2,1,0:T(8,128)} %all_to_all.20.refs_1_, f32[2,192,1]{2,1,0:T(8,128)} %copy.32.refs_2_, bf16[512,512]{1,0:T(8,128)(2,1)} %copy-done.9, bf16[512,512]{1,0:T(8,128)(2,1)} %copy-done.10, bf16[512,512]{1,0:T(8,128)(2,1)} %copy-done.7, ...), custom_call_target="tpu_custom_call" | custom-call | flops 2415919104 | bytes 4718592 | tf_op jit(solution)/shard_map/through_frequencies/pallas_call | solution.py:327
  439.4 9.1 %collective-permute-done.3.refs_3_ = f32[2,192,128]{2,1,0:T(8,128)S(1)} collective-permute-done((f32[2,192,128]{2,1,0:T(8,128)S(1)}, f32[2,192,128]{2,1,0:T(8,128)S(1)}, u32[]{:S(2)}, u32[]{:S(2)}) %collective-permute-start.3) | collective-permute-done | bytes 196640 | tf_op jit(solution)/shard_map/ppermute | solution.py:682
  460.9 5.4 collective-permute-done.6.refs_6_
  476.9 7.0 %collective-permute-done.21.refs_6_ = f32[2,400,128]{2,1,0:T(8,128)S(1)} collective-permute-done((f32[2,400,128]{2,1,0:T(8,128)}, f32[2,400,128]{2,1,0:T(8,128)S(1)}, u32[]{:S(2)}, u32[]{:S(2)}) %collective-permute-start.21) | collective-permute-done | bytes 409632 | tf_op jit(solution)/shard_map/ppermute | solution.py:682
  486.8 10.2 %collective-permute-done.22.refs_7_ = f32[2,400,128]{2,1,0:T(8,128)S(1)} collective-permute-done((f32[2,400,128]{2,1,0:T(8,128)}, f32[2,400,128]{2,1,0:T(8,128)S(1)}, u32[]{:S(2)}, u32[]{:S(2)}) %collective-permute-start.22) | collective-permute-done | bytes 409632 | tf_op jit(solution)/shard_map/ppermute | solution.py:682
  496.9 6.5 %collective-permute-start.10 = (f32[2,192,128]{2,1,0:T(8,128)}, f32[2,192,128]{2,1,0:T(8,128)}, u32[]{:S(2)}, u32[]{:S(2)}) collective-permute-start(f32[2,192,128]{2,1,0:T(8,128)} %get-tuple-element.40), channel_id=1, source_target_pairs={{0,9},{1,8},{2,11},{3,10},{4,13},{5,12},{6,15},{7,14},{8,1},{9,0},... | collective-permute-start | bytes 589832 | tf_op jit(solution)/shard_map/ppermute | solution.py:682
  503.4 6.5 %collective-permute-done.23.refs_8_ = f32[2,400,128]{2,1,0:T(8,128)S(1)} collective-permute-done((f32[2,400,128]{2,1,0:T(8,128)}, f32[2,400,128]{2,1,0:T(8,128)S(1)}, u32[]{:S(2)}, u32[]{:S(2)}) %collective-permute-start.23) | collective-permute-done | bytes 409632 | tf_op jit(solution)/shard_map/ppermute | solution.py:682
  531.4 14.9 %partial_back_along_y.1 = (f32[97,128,128]{2,1,0:T(8,128)}, f32[97,128,128]{2,1,0:T(8,128)}) custom-call(f32[6984,128]{1,0:T(8,128)} %copy-done.15, f32[8536,128]{1,0:T(8,128)} %copy-done.14, bf16[160,256]{1,0:T(8,128)(2,1)} %constant.227.clone.refs_2_, bf16[160,256]{1,0:T(8,128)(2,1)} %constant.228.clone.refs_3_), custom_call_target="tpu_custom_call" | custom-call | flops 4882169856 | bytes 25165824 | tf_op jit(solution)/shard_map/partial_back_along_y/pallas_call | solution.py:492
  550.8 6.4 %collective-permute-done.13.refs_13_ = f32[2,192,128]{2,1,0:T(8,128)S(1)} collective-permute-done((f32[2,192,128]{2,1,0:T(8,128)}, f32[2,192,128]{2,1,0:T(8,128)S(1)}, u32[]{:S(2)}, u32[]{:S(2)}) %collective-permute-start.13) | collective-permute-done | bytes 196640 | tf_op jit(solution)/shard_map/ppermute | solution.py:682
  561.5 6.2 %collective-permute-done.15.refs_15_ = f32[2,192,128]{2,1,0:T(8,128)S(1)} collective-permute-done((f32[2,192,128]{2,1,0:T(8,128)}, f32[2,192,128]{2,1,0:T(8,128)S(1)}, u32[]{:S(2)}, u32[]{:S(2)}) %collective-permute-start.15) | collective-permute-done | bytes 196640 | tf_op jit(solution)/shard_map/ppermute | solution.py:682
  574.8 26.1 %back_along_y.1 = f32[128,36864]{1,0:T(8,128)} custom-call(f32[6984,128]{1,0:T(8,128)} %copy-done.4, f32[97,128,128]{2,1,0:T(8,128)} %get-tuple-element.55.refs_1_.refs_4_.refs_7_, f32[97,128,128]{2,1,0:T(8,128)} %get-tuple-element.56.refs_2_.refs_5_.refs_8_, f32[6984,128]{1,0:T(8,128)} %copy-done.4, ...), custom_call_target="tpu_custom_call" | custom-call | flops 4882169856 | bytes 37748736 | tf_op jit(solution)/shard_map/back_along_y/pallas_call | solution.py:573
  (149 shorter events, 104.7 us)
Async XLA Ops:
  2.4 191.7 %collective-permute-start.1 = (f32[64,15360]{1,0:T(8,128)S(1)}, f32[64,15360]{1,0:T(8,128)S(1)}, u32[]{:S(2)}, u32[]{:S(2)}) collective-permute-start(f32[64,15360]{1,0:T(8,128)S(1)} %slice.29), channel_id=1, source_target_pairs={{0,15},{1,14},{2,13},{3,12},{4,11},{5,10},{6,9},{7,8},{8,7},{9,6},... | collective-permute-start | bytes 11796488 | tf_op jit(solution)/shard_map/ppermute | solution.py:654
  5.6 207.5 %collective-permute-start = (f32[64,3456]{1,0:T(8,128)S(1)}, f32[64,3456]{1,0:T(8,128)S(1)}, u32[]{:S(2)}, u32[]{:S(2)}) collective-permute-start(f32[64,3456]{1,0:T(8,128)S(1)} %slice.28), channel_id=1, source_target_pairs={{0,15},{1,14},{2,13},{3,12},{4,11},{5,10},{6,9},{7,8},{8,7},{9,6},... | collective-permute-start | bytes 2654216 | tf_op jit(solution)/shard_map/ppermute | solution.py:654
  220.1 41.5 %all-to-all-start = ((f32[16,192,128]{2,1,0:T(8,128)}), f32[16,192,128]{2,1,0:T(8,128)}, u32[]{:S(2)}, u32[]{:S(2)}) async-start(f32[16,192,128]{2,1,0:T(8,128)} %bitcast.5), calls=%async_computation | async-start | bytes 3145728 | tf_op jit(solution)/shard_map/all_to_all | solution.py:668
  395.7 125.1 %all-to-all-start.3 = ((f32[16,2,192,128]{3,2,1,0:T(8,128)}), f32[16,2,192,128]{3,2,1,0:T(8,128)S(1)}, u32[]{:S(2)}, u32[]{:S(2)}) async-start(f32[16,2,192,128]{3,2,1,0:T(8,128)} %through_frequencies.3), calls=%async_computation.3 | async-start | bytes 6291456 | tf_op jit(solution)/shard_map/all_to_all | solution.py:697
  423.3 46.2 %collective-permute-start.17 = (f32[2,400,128]{2,1,0:T(8,128)}, f32[2,400,128]{2,1,0:T(8,128)}, u32[]{:S(2)}, u32[]{:S(2)}) collective-permute-start(f32[2,400,128]{2,1,0:T(8,128)} %get-tuple-element.48), channel_id=1, source_target_pairs={{0,1},{1,0},{2,3},{3,2},{4,5},{5,4},{6,7},{7,6},{8,9},{9,8},{10,11... | collective-permute-start | bytes 1228808 | tf_op jit(solution)/shard_map/ppermute | solution.py:682
  423.7 45.8 %collective-permute-start.18 = (f32[2,400,128]{2,1,0:T(8,128)}, f32[2,400,128]{2,1,0:T(8,128)}, u32[]{:S(2)}, u32[]{:S(2)}) collective-permute-start(f32[2,400,128]{2,1,0:T(8,128)} %get-tuple-element.49), channel_id=1, source_target_pairs={{0,2},{1,3},{2,0},{3,1},{4,6},{5,7},{6,4},{7,5},{8,10},{9,11},{10,... | collective-permute-start | bytes 1228808 | tf_op jit(solution)/shard_map/ppermute | solution.py:682
  438.1 18.9 %collective-permute-start.4 = (f32[2,192,128]{2,1,0:T(8,128)S(1)}, f32[2,192,128]{2,1,0:T(8,128)S(1)}, u32[]{:S(2)}, u32[]{:S(2)}) collective-permute-start(f32[2,192,128]{2,1,0:T(8,128)S(1)} %get-tuple-element.34), channel_id=1, source_target_pairs={{0,3},{1,2},{2,1},{3,0},{4,7},{5,6},{6,5},{7,4},{8,11},{9,10},{10,... | collective-permute-start | bytes 589832 | tf_op jit(solution)/shard_map/ppermute | solution.py:682
  439.4 20.8 %collective-permute-start.5 = (f32[2,192,128]{2,1,0:T(8,128)S(1)}, f32[2,192,128]{2,1,0:T(8,128)S(1)}, u32[]{:S(2)}, u32[]{:S(2)}) collective-permute-start(f32[2,192,128]{2,1,0:T(8,128)S(1)} %get-tuple-element.35), channel_id=1, source_target_pairs={{0,4},{1,5},{2,6},{3,7},{4,0},{5,1},{6,2},{7,3},{8,12},{9,13},{10,... | collective-permute-start | bytes 589832 | tf_op jit(solution)/shard_map/ppermute | solution.py:682
  449.3 17.0 %collective-permute-start.6 = (f32[2,192,128]{2,1,0:T(8,128)S(1)}, f32[2,192,128]{2,1,0:T(8,128)S(1)}, u32[]{:S(2)}, u32[]{:S(2)}) collective-permute-start(f32[2,192,128]{2,1,0:T(8,128)S(1)} %get-tuple-element.36), channel_id=1, source_target_pairs={{0,5},{1,4},{2,7},{3,6},{4,1},{5,0},{6,3},{7,2},{8,13},{9,12},{10,... | collective-permute-start | bytes 589832 | tf_op jit(solution)/shard_map/ppermute | solution.py:682
  457.7 16.7 %collective-permute-start.19 = (f32[2,400,128]{2,1,0:T(8,128)}, f32[2,400,128]{2,1,0:T(8,128)S(1)}, u32[]{:S(2)}, u32[]{:S(2)}) collective-permute-start(f32[2,400,128]{2,1,0:T(8,128)} %copy-done.41), channel_id=1, source_target_pairs={{0,3},{1,2},{2,1},{3,0},{4,7},{5,6},{6,5},{7,4},{8,11},{9,10},{10,... | collective-permute-start | bytes 1228808 | tf_op jit(solution)/shard_map/ppermute | solution.py:682
  460.9 14.3 %collective-permute-start.20 = (f32[2,400,128]{2,1,0:T(8,128)}, f32[2,400,128]{2,1,0:T(8,128)S(1)}, u32[]{:S(2)}, u32[]{:S(2)}) collective-permute-start(f32[2,400,128]{2,1,0:T(8,128)} %copy-done.40), channel_id=1, source_target_pairs={{0,4},{1,5},{2,6},{3,7},{4,0},{5,1},{6,2},{7,3},{8,12},{9,13},{10,... | collective-permute-start | bytes 1228808 | tf_op jit(solution)/shard_map/ppermute | solution.py:682
  467.0 17.0 %collective-permute-start.21 = (f32[2,400,128]{2,1,0:T(8,128)}, f32[2,400,128]{2,1,0:T(8,128)S(1)}, u32[]{:S(2)}, u32[]{:S(2)}) collective-permute-start(f32[2,400,128]{2,1,0:T(8,128)} %copy-done.39), channel_id=1, source_target_pairs={{0,5},{1,4},{2,7},{3,6},{4,1},{5,0},{6,3},{7,2},{8,13},{9,12},{10,... | collective-permute-start | bytes 1228808 | tf_op jit(solution)/shard_map/ppermute | solution.py:682
  469.4 27.5 %collective-permute-start.22 = (f32[2,400,128]{2,1,0:T(8,128)}, f32[2,400,128]{2,1,0:T(8,128)S(1)}, u32[]{:S(2)}, u32[]{:S(2)}) collective-permute-start(f32[2,400,128]{2,1,0:T(8,128)} %copy-done.38), channel_id=1, source_target_pairs={{0,6},{1,7},{2,4},{3,5},{4,2},{5,3},{6,0},{7,1},{8,14},{9,15},{10,... | collective-permute-start | bytes 1228808 | tf_op jit(solution)/shard_map/ppermute | solution.py:682
  469.5 40.5 %collective-permute-start.23 = (f32[2,400,128]{2,1,0:T(8,128)}, f32[2,400,128]{2,1,0:T(8,128)S(1)}, u32[]{:S(2)}, u32[]{:S(2)}) collective-permute-start(f32[2,400,128]{2,1,0:T(8,128)} %copy-done.37), channel_id=1, source_target_pairs={{0,7},{1,6},{2,5},{3,4},{4,3},{5,2},{6,1},{7,0},{8,15},{9,14},{10,... | collective-permute-start | bytes 1228808 | tf_op jit(solution)/shard_map/ppermute | solution.py:682
  474.4 50.6 %collective-permute-start.7 = (f32[2,192,128]{2,1,0:T(8,128)}, f32[2,192,128]{2,1,0:T(8,128)}, u32[]{:S(2)}, u32[]{:S(2)}) collective-permute-start(f32[2,192,128]{2,1,0:T(8,128)} %get-tuple-element.37), channel_id=1, source_target_pairs={{0,6},{1,7},{2,4},{3,5},{4,2},{5,3},{6,0},{7,1},{8,14},{9,15},{10,... | collective-permute-start | bytes 589832 | tf_op jit(solution)/shard_map/ppermute | solution.py:682
  475.2 50.0 %collective-permute-start.8 = (f32[2,192,128]{2,1,0:T(8,128)}, f32[2,192,128]{2,1,0:T(8,128)}, u32[]{:S(2)}, u32[]{:S(2)}) collective-permute-start(f32[2,192,128]{2,1,0:T(8,128)} %get-tuple-element.38), channel_id=1, source_target_pairs={{0,7},{1,6},{2,5},{3,4},{4,3},{5,2},{6,1},{7,0},{8,15},{9,14},{10,... | collective-permute-start | bytes 589832 | tf_op jit(solution)/shard_map/ppermute | solution.py:682
  484.0 42.5 %collective-permute-start.9 = (f32[2,192,128]{2,1,0:T(8,128)}, f32[2,192,128]{2,1,0:T(8,128)}, u32[]{:S(2)}, u32[]{:S(2)}) collective-permute-start(f32[2,192,128]{2,1,0:T(8,128)} %get-tuple-element.39), channel_id=1, source_target_pairs={{0,8},{1,9},{2,10},{3,11},{4,12},{5,13},{6,14},{7,15},{8,0},{9,1},... | collective-permute-start | bytes 589832 | tf_op jit(solution)/shard_map/ppermute | solution.py:682
  496.9 30.1 %collective-permute-start.10 = (f32[2,192,128]{2,1,0:T(8,128)}, f32[2,192,128]{2,1,0:T(8,128)}, u32[]{:S(2)}, u32[]{:S(2)}) collective-permute-start(f32[2,192,128]{2,1,0:T(8,128)} %get-tuple-element.40), channel_id=1, source_target_pairs={{0,9},{1,8},{2,11},{3,10},{4,13},{5,12},{6,15},{7,14},{8,1},{9,0},... | collective-permute-start | bytes 589832 | tf_op jit(solution)/shard_map/ppermute | solution.py:682
  509.9 20.0 %collective-permute-start.11 = (f32[2,192,128]{2,1,0:T(8,128)}, f32[2,192,128]{2,1,0:T(8,128)}, u32[]{:S(2)}, u32[]{:S(2)}) collective-permute-start(f32[2,192,128]{2,1,0:T(8,128)} %get-tuple-element.41), channel_id=1, source_target_pairs={{0,10},{1,11},{2,8},{3,9},{4,14},{5,15},{6,12},{7,13},{8,2},{9,3},... | collective-permute-start | bytes 589832 | tf_op jit(solution)/shard_map/ppermute | solution.py:682
  525.0 25.8 %collective-permute-start.12 = (f32[2,192,128]{2,1,0:T(8,128)}, f32[2,192,128]{2,1,0:T(8,128)S(1)}, u32[]{:S(2)}, u32[]{:S(2)}) collective-permute-start(f32[2,192,128]{2,1,0:T(8,128)} %get-tuple-element.42), channel_id=1, source_target_pairs={{0,11},{1,10},{2,9},{3,8},{4,15},{5,14},{6,13},{7,12},{8,3},{9,2},... | collective-permute-start | bytes 589832 | tf_op jit(solution)/shard_map/ppermute | solution.py:682
  525.2 32.1 %collective-permute-start.13 = (f32[2,192,128]{2,1,0:T(8,128)}, f32[2,192,128]{2,1,0:T(8,128)S(1)}, u32[]{:S(2)}, u32[]{:S(2)}) collective-permute-start(f32[2,192,128]{2,1,0:T(8,128)} %get-tuple-element.43), channel_id=1, source_target_pairs={{0,12},{1,13},{2,14},{3,15},{4,8},{5,9},{6,10},{7,11},{8,4},{9,5},... | collective-permute-start | bytes 589832 | tf_op jit(solution)/shard_map/ppermute | solution.py:682
  526.5 35.0 %collective-permute-start.14 = (f32[2,192,128]{2,1,0:T(8,128)}, f32[2,192,128]{2,1,0:T(8,128)S(1)}, u32[]{:S(2)}, u32[]{:S(2)}) collective-permute-start(f32[2,192,128]{2,1,0:T(8,128)} %get-tuple-element.44), channel_id=1, source_target_pairs={{0,13},{1,12},{2,15},{3,14},{4,9},{5,8},{6,11},{7,10},{8,5},{9,4},... | collective-permute-start | bytes 589832 | tf_op jit(solution)/shard_map/ppermute | solution.py:682
  527.1 40.6 %collective-permute-start.15 = (f32[2,192,128]{2,1,0:T(8,128)}, f32[2,192,128]{2,1,0:T(8,128)S(1)}, u32[]{:S(2)}, u32[]{:S(2)}) collective-permute-start(f32[2,192,128]{2,1,0:T(8,128)} %get-tuple-element.45), channel_id=1, source_target_pairs={{0,14},{1,15},{2,12},{3,13},{4,10},{5,11},{6,8},{7,9},{8,6},{9,7},... | collective-permute-start | bytes 589832 | tf_op jit(solution)/shard_map/ppermute | solution.py:682
  530.0 39.2 %collective-permute-start.16 = (f32[2,192,128]{2,1,0:T(8,128)}, f32[2,192,128]{2,1,0:T(8,128)S(1)}, u32[]{:S(2)}, u32[]{:S(2)}) collective-permute-start(f32[2,192,128]{2,1,0:T(8,128)} %get-tuple-element.46), channel_id=1, source_target_pairs={{0,15},{1,14},{2,13},{3,12},{4,11},{5,10},{6,9},{7,8},{8,7},{9,6},... | collective-permute-start | bytes 589832 | tf_op jit(solution)/shard_map/ppermute | solution.py:682
  (44 other events, 2496.2 us)

commit v4 on v3

--- a/solution.py
+++ b/solution.py
@@ -467,11 +467,19 @@
     return table_halves(np.concatenate(tables, axis=0))
 
 
-X_STEP = 32
+X_STEP = 16
 
 
 def turned_lines(parts, table):
     result = product3(halves_of(jnp.concatenate(parts, axis=0).T), table, NN)
+    cosines, sines = result[:, :LANES], result[:, LANES:]
+    return cosines - sines, cosines + sines
+
+
+def packed_lines(lines, table):
+    high = lines.astype(bf16).astype(f32)
+    stacked = jnp.concatenate([high, high, lines - high], axis=0)
+    result = product(stacked.T.astype(bf16), table, NN)
     cosines, sines = result[:, :LANES], result[:, LANES:]
     return cosines - sines, cosines + sines
 
@@ -505,16 +513,16 @@
 
 def back_y_kernel(depth, *refs):
     halves, heads, zeroth = refs[:3], refs[3:6], refs[6:9]
-    high_ref, low_ref, own_ref, out_ref, minus_ref, plus_ref = refs[9:]
+    table_ref, own_ref, out_ref, minus_ref, plus_ref = refs[9:]
     step, side = pl.program_id(0), pl.program_id(1)
-    table = (high_ref[...], low_ref[...])
+    table = table_ref[...]
     lane = lax.broadcasted_iota(jnp.int32, (LANES, LANES), 1)
     turned_lane = (LANES // 2 - lane) & (LANES - 1)
     ring = 2 * X_STEP
 
     def fill(source, s, line):
         z_ref, early_minus_ref, early_plus_ref = source
-        minus, plus = turned_lines([z_ref[s * depth : (s + 1) * depth, :]], table)
+        minus, plus = packed_lines(z_ref[s * depth : (s + 1) * depth, :], table)
         slot = line & (ring - 1)
         minus_ref[slot] = minus + early_minus_ref[s]
         plus_ref[slot] = plus + early_plus_ref[s]
@@ -558,6 +566,7 @@
 def back_along_y(propagator, early, last, first, count):
     slab, sites = propagator.shape
     high, low = back_y_table(first, [count])
+    table = jnp.concatenate([high, low, high], axis=0)
     depth = back_x_depth(count)[1]
     width = X_STEP * L
     steps = HALF_L // X_STEP
@@ -576,7 +585,7 @@
         in_specs=lines(half, lambda i, j: jnp.minimum(2 * i + 1 + j, 2 * steps - 1))
         + lines(half, lambda i, j: 0)
         + lines(1, lambda i, j: HALF_L)
-        + [whole(high), whole(low), moving],
+        + [whole(table), moving],
         out_specs=moving,
         out_shape=jax.ShapeDtypeStruct((slab, sites), f32),
         scratch_shapes=[pltpu.VMEM((2 * X_STEP, LANES, LANES), f32)] * 2,
@@ -585,11 +594,11 @@
         ),
         interpret=INTERPRET,
         name="back_along_y",
-    )(*sources, *sources, *sources, high, low, propagator)
+    )(*sources, *sources, *sources, table, propagator)
 
 
 CUTS = (0, 40, KEPT // 2 + 1)
-CHUNKS = ((32, 8, 96, False), (33, 12, 200, True), (32, 8, 96, False))
+CHUNKS = ((32, 8, 64, False), (33, 12, 104, True), (32, 8, 64, False))
 
 
 def token(x):

time: 604 us -> 609 us (level)
  Pallas kernels: 103 us -> 112 us
    pallas_call x3, Pallas kernels: 29.6 us -> 38 us  [through_frequencies(): pl.pallas_call(lambda *refs: frequency_kernel(both_sides, *refs), grid=(-...]
  transfers between devices with their start and end apart: 26 -> 26, of which waited for: 16 -> 15; matrix products, arithmetic and copies ran while one was open for 4% -> 4% of each run, Pallas kernels for 9% -> 10%
where the time goes in v4:
time: 609 us; the launch traced here: 607 us
  waiting for transfers between devices  268 us (44%)
  blocking collectives  118 us (19%)
  Pallas kernels  112 us (18%)
  starting transfers between devices  50.1 us (8%)
  local copies, waits for them, and re-layouts  41.1 us (7%)
  other arithmetic  16.7 us (3%)
    ppermute x2, waiting for transfers between devices, with_kernels(): lax.ppermute(propagator[half:, first * PAIR:last * PAIR], 'tau', partner)  177 us
    all_to_all x2, blocking collectives, with_kernels(): lax.all_to_all(pol_mom, 'tau', split_axis=0, concat_axis=0, tiled=True)  118 us
    ppermute x22, waiting for transfers between devices, exchanged(): lax.ppermute(blocks[k], 'tau', [(d, d ^ k) for d in range(devices)])  63.9 us
    pallas_call x3, Pallas kernels, through_frequencies(): pl.pallas_call(lambda *refs: frequency_kernel(both_sides, *refs), grid=(-...  38 us
    ppermute x22, starting transfers between devices, exchanged(): lax.ppermute(blocks[k], 'tau', [(d, d ^ k) for d in range(devices)])  36.5 us
    unnamed x84, local copies, waits for them, and re-layouts  30.9 us
    all_to_all x1, waiting for transfers between devices, with_kernels(): lax.all_to_all(pol_mom, 'tau', split_axis=0, concat_axis=0, tiled=True)  26.9 us
    pallas_call x1, Pallas kernels, back_along_y(): pl.pallas_call(lambda *refs: back_y_kernel(depth, *refs), grid=(steps, 2)...  25.9 us
  transfers between devices with their start and end apart: 26, of which 15 were waited for; matrix products, arithmetic and copies ran while one was open for 4% of the time, Pallas kernels for 10%

profile of v4, /device:TPU:11, one launch (start us, length us, event | category | flops | bytes accessed | tf_op | source)
XLA Modules:
  0.0 607.5 jit_solution(15889249002916417601)
XLA Ops:
  6.5 16.2 %fusion.1 = (bf16[512,512]{1,0:T(8,128)(2,1)S(1)}, bf16[512,512]{1,0:T(8,128)(2,1)S(1)}, bf16[512,512]{1,0:T(8,128)(2,1)S(1)}, bf16[512,512]{1,0:T(8,128)(2,1)S(...) fusion(s32[512]{0:T(512)S(1)} %get-tuple-element.70, ...), kind=kLoop, calls=%fused_computation.29 | loop fusion | flops 19922944 | bytes 4200448 | tf_op jit(solution)/shard_map/convert_element_type | solution.py:649
  22.8 171.4 %collective-permute-done.1.refs_1_ = f32[64,15360]{1,0:T(8,128)S(1)} collective-permute-done((f32[64,15360]{1,0:T(8,128)S(1)}, f32[64,15360]{1,0:T(8,128)S(1)}, u32[]{:S(2)}, u32[]{:S(2)}) %collective-permute-start.1) | collective-permute-done | bytes 3932192 | tf_op jit(solution)/shard_map/ppermute | solution.py:663
  194.2 6.4 %copy-done = f32[128,36864]{1,0:T(8,128)S(1)} copy-done((f32[128,36864]{1,0:T(8,128)S(1)}, f32[128,36864]{1,0:T(8,128)}, u32[]{:S(2)}) %copy-start) | copy-done | bytes 18874392
  200.6 6.6 %bubble_along_y.2.refs_5_ = f32[56,256,128]{2,1,0:T(8,128)S(1)} custom-call(f32[128,36864]{1,0:T(8,128)S(1)} %copy-done, f32[64,15360]{1,0:T(8,128)S(1)} %collective-permute-done.1.refs_1_, bf16[64,64]{1,0:T(8,128)(2,1)S(1)} %copy-done.35, bf16[256,512]{1,0:T(8,128)(2,1)S(1)} %copy-done.18, bf16[256,512]{1,0:T(8,128)(2,1)S(1)} %copy-done.17, ...), custom_call_target="tpu_custom_call" | custom-call | flops 4026531840 | bytes 11796480 | tf_op jit(solution)/shard_map/bubble_along_y/pallas_call | solution.py:204
  207.3 5.8 collective-permute-done.refs_1_
  215.8 4.2 along_x.3
  220.1 5.2 all-to-all-start
  234.7 26.9 %all-to-all-done.refs_1_ = f32[16,192,128]{2,1,0:T(8,128)} async-done(((f32[16,192,128]{2,1,0:T(8,128)}), f32[16,192,128]{2,1,0:T(8,128)}, u32[]{:S(2)}, u32[]{:S(2)}) %all-to-all-start) | async-done | bytes 1572896 | tf_op jit(solution)/shard_map/all_to_all | solution.py:677
  261.6 11.9 %through_frequencies.3 = f32[16,2,192,128]{3,2,1,0:T(8,128)} custom-call(f32[1]{0:T(128)} %bitcast.1.refs_0_, f32[16,192,128]{2,1,0:T(8,128)} %all-to-all-done.refs_1_, f32[2,192,1]{2,1,0:T(8,128)} %copy.30.refs_2_, bf16[512,512]{1,0:T(8,128)(2,1)} %copy-done.9, bf16[512,512]{1,0:T(8,128)(2,1)} %copy-done.10, bf16[512,512]{1,0:T(8,128)(2,1)} %copy-done.7, ...), custom_call_target="tpu_custom_call" | custom-call | flops 2415919104 | bytes 4718592 | tf_op jit(solution)/shard_map/through_frequencies/pallas_call | solution.py:327
  280.2 40.7 %all_to_all.20.refs_1_ = f32[16,192,128]{2,1,0:T(8,128)} all-to-all(f32[16,192,128]{2,1,0:T(8,128)S(1)} %bitcast.30), channel_id=1, replica_groups=mesh['grp'=2,'tau'=16] {'tau'}, dimensions={0} | all-to-all | bytes 3145728 | tf_op jit(solution)/shard_map/all_to_all | solution.py:677
  321.0 77.4 %all_to_all.21.refs_1_ = f32[16,400,128]{2,1,0:T(8,128)} all-to-all(f32[16,400,128]{2,1,0:T(8,128)S(1)} %bitcast.29), channel_id=1, replica_groups=mesh['grp'=2,'tau'=16] {'tau'}, dimensions={0} | all-to-all | bytes 6553600 | tf_op jit(solution)/shard_map/all_to_all | solution.py:677
  398.4 5.6 all-to-all-start.3
  406.1 14.1 %through_frequencies.4.w_ref = f32[8,2,400,128]{3,2,1,0:T(8,128)} custom-call(f32[1]{0:T(128)} %bitcast.1.refs_0_, f32[16,400,128]{2,1,0:T(8,128)} %all_to_all.21.refs_1_, f32[2,400,1]{2,1,0:T(8,128)} %copy.31.refs_2_, bf16[512,512]{1,0:T(8,128)(2,1)} %copy-done.9, bf16[512,512]{1,0:T(8,128)(2,1)} %copy-done.10, bf16[512,512]{1,0:T(8,128)(2,1)} %copy-done.7, ...), custom_call_target="tpu_custom_call" | custom-call | flops 5033164800 | bytes 9830400 | tf_op jit(solution)/shard_map/through_frequencies/pallas_call | solution.py:327
  429.7 11.9 %through_frequencies.5.w_ref = f32[16,2,192,128]{3,2,1,0:T(8,128)} custom-call(f32[1]{0:T(128)} %bitcast.1.refs_0_, f32[16,192,128]{2,1,0:T(8,128)} %all_to_all.20.refs_1_, f32[2,192,1]{2,1,0:T(8,128)} %copy.32.refs_2_, bf16[512,512]{1,0:T(8,128)(2,1)} %copy-done.9, bf16[512,512]{1,0:T(8,128)(2,1)} %copy-done.10, bf16[512,512]{1,0:T(8,128)(2,1)} %copy-done.7, ...), custom_call_target="tpu_custom_call" | custom-call | flops 2415919104 | bytes 4718592 | tf_op jit(solution)/shard_map/through_frequencies/pallas_call | solution.py:327
  447.9 10.3 %collective-permute-done.3.refs_3_ = f32[2,192,128]{2,1,0:T(8,128)S(1)} collective-permute-done((f32[2,192,128]{2,1,0:T(8,128)S(1)}, f32[2,192,128]{2,1,0:T(8,128)S(1)}, u32[]{:S(2)}, u32[]{:S(2)}) %collective-permute-start.3) | collective-permute-done | bytes 196640 | tf_op jit(solution)/shard_map/ppermute | solution.py:691
  481.9 6.3 %collective-permute-done.21.refs_6_ = f32[2,400,128]{2,1,0:T(8,128)S(1)} collective-permute-done((f32[2,400,128]{2,1,0:T(8,128)}, f32[2,400,128]{2,1,0:T(8,128)S(1)}, u32[]{:S(2)}, u32[]{:S(2)}) %collective-permute-start.21) | collective-permute-done | bytes 409632 | tf_op jit(solution)/shard_map/ppermute | solution.py:691
  490.6 8.8 %collective-permute-done.22.refs_7_ = f32[2,400,128]{2,1,0:T(8,128)S(1)} collective-permute-done((f32[2,400,128]{2,1,0:T(8,128)}, f32[2,400,128]{2,1,0:T(8,128)S(1)}, u32[]{:S(2)}, u32[]{:S(2)}) %collective-permute-start.22) | collective-permute-done | bytes 409632 | tf_op jit(solution)/shard_map/ppermute | solution.py:691
  499.4 7.0 %collective-permute-start.10 = (f32[2,192,128]{2,1,0:T(8,128)}, f32[2,192,128]{2,1,0:T(8,128)}, u32[]{:S(2)}, u32[]{:S(2)}) collective-permute-start(f32[2,192,128]{2,1,0:T(8,128)} %get-tuple-element.40), channel_id=1, source_target_pairs={{0,9},{1,8},{2,11},{3,10},{4,13},{5,12},{6,15},{7,14},{8,1},{9,0},... | collective-permute-start | bytes 589832 | tf_op jit(solution)/shard_map/ppermute | solution.py:691
  506.4 6.0 collective-permute-done.23.refs_8_
  512.4 5.1 collective-permute-start.11
  535.9 14.9 %partial_back_along_y.1 = (f32[97,128,128]{2,1,0:T(8,128)}, f32[97,128,128]{2,1,0:T(8,128)}) custom-call(f32[6984,128]{1,0:T(8,128)} %copy-done.15, f32[8536,128]{1,0:T(8,128)} %copy-done.14, bf16[160,256]{1,0:T(8,128)(2,1)} %constant.227.clone.refs_2_, bf16[160,256]{1,0:T(8,128)(2,1)} %constant.228.clone.refs_3_), custom_call_target="tpu_custom_call" | custom-call | flops 4882169856 | bytes 25165824 | tf_op jit(solution)/shard_map/partial_back_along_y/pallas_call | solution.py:500
  560.1 6.3 %collective-permute-done.14.refs_14_ = f32[2,192,128]{2,1,0:T(8,128)S(1)} collective-permute-done((f32[2,192,128]{2,1,0:T(8,128)}, f32[2,192,128]{2,1,0:T(8,128)S(1)}, u32[]{:S(2)}, u32[]{:S(2)}) %collective-permute-start.14) | collective-permute-done | bytes 196640 | tf_op jit(solution)/shard_map/ppermute | solution.py:691
  566.5 5.2 collective-permute-done.15.refs_15_
  581.5 25.9 %back_along_y.1 = f32[128,36864]{1,0:T(8,128)} custom-call(f32[6984,128]{1,0:T(8,128)} %copy-done.4, f32[97,128,128]{2,1,0:T(8,128)} %get-tuple-element.55.refs_1_.refs_4_.refs_7_, f32[97,128,128]{2,1,0:T(8,128)} %get-tuple-element.56.refs_2_.refs_5_.refs_8_, f32[6984,128]{1,0:T(8,128)} %copy-done.4, ...), custom_call_target="tpu_custom_call" | custom-call | flops 4882169856 | bytes 37748736 | tf_op jit(solution)/shard_map/back_along_y/pallas_call | solution.py:582
  (149 shorter events, 105.3 us)
Async XLA Ops:
  2.4 191.7 %collective-permute-start.1 = (f32[64,15360]{1,0:T(8,128)S(1)}, f32[64,15360]{1,0:T(8,128)S(1)}, u32[]{:S(2)}, u32[]{:S(2)}) collective-permute-start(f32[64,15360]{1,0:T(8,128)S(1)} %slice.29), channel_id=1, source_target_pairs={{0,15},{1,14},{2,13},{3,12},{4,11},{5,10},{6,9},{7,8},{8,7},{9,6},... | collective-permute-start | bytes 11796488 | tf_op jit(solution)/shard_map/ppermute | solution.py:663
  5.6 207.5 %collective-permute-start = (f32[64,3456]{1,0:T(8,128)S(1)}, f32[64,3456]{1,0:T(8,128)S(1)}, u32[]{:S(2)}, u32[]{:S(2)}) collective-permute-start(f32[64,3456]{1,0:T(8,128)S(1)} %slice.28), channel_id=1, source_target_pairs={{0,15},{1,14},{2,13},{3,12},{4,11},{5,10},{6,9},{7,8},{8,7},{9,6},... | collective-permute-start | bytes 2654216 | tf_op jit(solution)/shard_map/ppermute | solution.py:663
  220.1 41.5 %all-to-all-start = ((f32[16,192,128]{2,1,0:T(8,128)}), f32[16,192,128]{2,1,0:T(8,128)}, u32[]{:S(2)}, u32[]{:S(2)}) async-start(f32[16,192,128]{2,1,0:T(8,128)} %bitcast.5), calls=%async_computation | async-start | bytes 3145728 | tf_op jit(solution)/shard_map/all_to_all | solution.py:677
  398.4 126.2 %all-to-all-start.3 = ((f32[16,2,192,128]{3,2,1,0:T(8,128)}), f32[16,2,192,128]{3,2,1,0:T(8,128)S(1)}, u32[]{:S(2)}, u32[]{:S(2)}) async-start(f32[16,2,192,128]{3,2,1,0:T(8,128)} %through_frequencies.3), calls=%async_computation.3 | async-start | bytes 6291456 | tf_op jit(solution)/shard_map/all_to_all | solution.py:706
  429.1 43.1 %collective-permute-start.17 = (f32[2,400,128]{2,1,0:T(8,128)}, f32[2,400,128]{2,1,0:T(8,128)}, u32[]{:S(2)}, u32[]{:S(2)}) collective-permute-start(f32[2,400,128]{2,1,0:T(8,128)} %get-tuple-element.48), channel_id=1, source_target_pairs={{0,1},{1,0},{2,3},{3,2},{4,5},{5,4},{6,7},{7,6},{8,9},{9,8},{10,11... | collective-permute-start | bytes 1228808 | tf_op jit(solution)/shard_map/ppermute | solution.py:691
  429.5 42.7 %collective-permute-start.18 = (f32[2,400,128]{2,1,0:T(8,128)}, f32[2,400,128]{2,1,0:T(8,128)}, u32[]{:S(2)}, u32[]{:S(2)}) collective-permute-start(f32[2,400,128]{2,1,0:T(8,128)} %get-tuple-element.49), channel_id=1, source_target_pairs={{0,2},{1,3},{2,0},{3,1},{4,6},{5,7},{6,4},{7,5},{8,10},{9,11},{10,... | collective-permute-start | bytes 1228808 | tf_op jit(solution)/shard_map/ppermute | solution.py:691
  445.4 12.8 %collective-permute-start.3 = (f32[2,192,128]{2,1,0:T(8,128)S(1)}, f32[2,192,128]{2,1,0:T(8,128)S(1)}, u32[]{:S(2)}, u32[]{:S(2)}) collective-permute-start(f32[2,192,128]{2,1,0:T(8,128)S(1)} %get-tuple-element.33), channel_id=1, source_target_pairs={{0,2},{1,3},{2,0},{3,1},{4,6},{5,7},{6,4},{7,5},{8,10},{9,11},{10,... | collective-permute-start | bytes 589832 | tf_op jit(solution)/shard_map/ppermute | solution.py:691
  446.6 15.9 %collective-permute-start.4 = (f32[2,192,128]{2,1,0:T(8,128)S(1)}, f32[2,192,128]{2,1,0:T(8,128)S(1)}, u32[]{:S(2)}, u32[]{:S(2)}) collective-permute-start(f32[2,192,128]{2,1,0:T(8,128)S(1)} %get-tuple-element.34), channel_id=1, source_target_pairs={{0,3},{1,2},{2,1},{3,0},{4,7},{5,6},{6,5},{7,4},{8,11},{9,10},{10,... | collective-permute-start | bytes 589832 | tf_op jit(solution)/shard_map/ppermute | solution.py:691
  447.8 15.6 %collective-permute-start.5 = (f32[2,192,128]{2,1,0:T(8,128)S(1)}, f32[2,192,128]{2,1,0:T(8,128)S(1)}, u32[]{:S(2)}, u32[]{:S(2)}) collective-permute-start(f32[2,192,128]{2,1,0:T(8,128)S(1)} %get-tuple-element.35), channel_id=1, source_target_pairs={{0,4},{1,5},{2,6},{3,7},{4,0},{5,1},{6,2},{7,3},{8,12},{9,13},{10,... | collective-permute-start | bytes 589832 | tf_op jit(solution)/shard_map/ppermute | solution.py:691
  463.2 16.1 %collective-permute-start.19 = (f32[2,400,128]{2,1,0:T(8,128)}, f32[2,400,128]{2,1,0:T(8,128)S(1)}, u32[]{:S(2)}, u32[]{:S(2)}) collective-permute-start(f32[2,400,128]{2,1,0:T(8,128)} %copy-done.41), channel_id=1, source_target_pairs={{0,3},{1,2},{2,1},{3,0},{4,7},{5,6},{6,5},{7,4},{8,11},{9,10},{10,... | collective-permute-start | bytes 1228808 | tf_op jit(solution)/shard_map/ppermute | solution.py:691
  464.2 15.2 %collective-permute-start.20 = (f32[2,400,128]{2,1,0:T(8,128)}, f32[2,400,128]{2,1,0:T(8,128)S(1)}, u32[]{:S(2)}, u32[]{:S(2)}) collective-permute-start(f32[2,400,128]{2,1,0:T(8,128)} %copy-done.40), channel_id=1, source_target_pairs={{0,4},{1,5},{2,6},{3,7},{4,0},{5,1},{6,2},{7,3},{8,12},{9,13},{10,... | collective-permute-start | bytes 1228808 | tf_op jit(solution)/shard_map/ppermute | solution.py:691
  469.7 18.5 %collective-permute-start.21 = (f32[2,400,128]{2,1,0:T(8,128)}, f32[2,400,128]{2,1,0:T(8,128)S(1)}, u32[]{:S(2)}, u32[]{:S(2)}) collective-permute-start(f32[2,400,128]{2,1,0:T(8,128)} %copy-done.39), channel_id=1, source_target_pairs={{0,5},{1,4},{2,7},{3,6},{4,1},{5,0},{6,3},{7,2},{8,13},{9,12},{10,... | collective-permute-start | bytes 1228808 | tf_op jit(solution)/shard_map/ppermute | solution.py:691
  472.2 27.3 %collective-permute-start.22 = (f32[2,400,128]{2,1,0:T(8,128)}, f32[2,400,128]{2,1,0:T(8,128)S(1)}, u32[]{:S(2)}, u32[]{:S(2)}) collective-permute-start(f32[2,400,128]{2,1,0:T(8,128)} %copy-done.38), channel_id=1, source_target_pairs={{0,6},{1,7},{2,4},{3,5},{4,2},{5,3},{6,0},{7,1},{8,14},{9,15},{10,... | collective-permute-start | bytes 1228808 | tf_op jit(solution)/shard_map/ppermute | solution.py:691
  472.2 40.3 %collective-permute-start.23 = (f32[2,400,128]{2,1,0:T(8,128)}, f32[2,400,128]{2,1,0:T(8,128)S(1)}, u32[]{:S(2)}, u32[]{:S(2)}) collective-permute-start(f32[2,400,128]{2,1,0:T(8,128)} %copy-done.37), channel_id=1, source_target_pairs={{0,7},{1,6},{2,5},{3,4},{4,3},{5,2},{6,1},{7,0},{8,15},{9,14},{10,... | collective-permute-start | bytes 1228808 | tf_op jit(solution)/shard_map/ppermute | solution.py:691
  479.3 49.6 %collective-permute-start.7 = (f32[2,192,128]{2,1,0:T(8,128)}, f32[2,192,128]{2,1,0:T(8,128)}, u32[]{:S(2)}, u32[]{:S(2)}) collective-permute-start(f32[2,192,128]{2,1,0:T(8,128)} %get-tuple-element.37), channel_id=1, source_target_pairs={{0,6},{1,7},{2,4},{3,5},{4,2},{5,3},{6,0},{7,1},{8,14},{9,15},{10,... | collective-permute-start | bytes 589832 | tf_op jit(solution)/shard_map/ppermute | solution.py:691
  479.3 52.1 %collective-permute-start.8 = (f32[2,192,128]{2,1,0:T(8,128)}, f32[2,192,128]{2,1,0:T(8,128)}, u32[]{:S(2)}, u32[]{:S(2)}) collective-permute-start(f32[2,192,128]{2,1,0:T(8,128)} %get-tuple-element.38), channel_id=1, source_target_pairs={{0,7},{1,6},{2,5},{3,4},{4,3},{5,2},{6,1},{7,0},{8,15},{9,14},{10,... | collective-permute-start | bytes 589832 | tf_op jit(solution)/shard_map/ppermute | solution.py:691
  488.2 43.2 %collective-permute-start.9 = (f32[2,192,128]{2,1,0:T(8,128)}, f32[2,192,128]{2,1,0:T(8,128)}, u32[]{:S(2)}, u32[]{:S(2)}) collective-permute-start(f32[2,192,128]{2,1,0:T(8,128)} %get-tuple-element.39), channel_id=1, source_target_pairs={{0,8},{1,9},{2,10},{3,11},{4,12},{5,13},{6,14},{7,15},{8,0},{9,1},... | collective-permute-start | bytes 589832 | tf_op jit(solution)/shard_map/ppermute | solution.py:691
  499.4 34.1 %collective-permute-start.10 = (f32[2,192,128]{2,1,0:T(8,128)}, f32[2,192,128]{2,1,0:T(8,128)}, u32[]{:S(2)}, u32[]{:S(2)}) collective-permute-start(f32[2,192,128]{2,1,0:T(8,128)} %get-tuple-element.40), channel_id=1, source_target_pairs={{0,9},{1,8},{2,11},{3,10},{4,13},{5,12},{6,15},{7,14},{8,1},{9,0},... | collective-permute-start | bytes 589832 | tf_op jit(solution)/shard_map/ppermute | solution.py:691
  512.4 21.5 %collective-permute-start.11 = (f32[2,192,128]{2,1,0:T(8,128)}, f32[2,192,128]{2,1,0:T(8,128)}, u32[]{:S(2)}, u32[]{:S(2)}) collective-permute-start(f32[2,192,128]{2,1,0:T(8,128)} %get-tuple-element.41), channel_id=1, source_target_pairs={{0,10},{1,11},{2,8},{3,9},{4,14},{5,15},{6,12},{7,13},{8,2},{9,3},... | collective-permute-start | bytes 589832 | tf_op jit(solution)/shard_map/ppermute | solution.py:691
  528.9 27.0 %collective-permute-start.12 = (f32[2,192,128]{2,1,0:T(8,128)}, f32[2,192,128]{2,1,0:T(8,128)S(1)}, u32[]{:S(2)}, u32[]{:S(2)}) collective-permute-start(f32[2,192,128]{2,1,0:T(8,128)} %get-tuple-element.42), channel_id=1, source_target_pairs={{0,11},{1,10},{2,9},{3,8},{4,15},{5,14},{6,13},{7,12},{8,3},{9,2},... | collective-permute-start | bytes 589832 | tf_op jit(solution)/shard_map/ppermute | solution.py:691
  531.4 28.7 %collective-permute-start.13 = (f32[2,192,128]{2,1,0:T(8,128)}, f32[2,192,128]{2,1,0:T(8,128)S(1)}, u32[]{:S(2)}, u32[]{:S(2)}) collective-permute-start(f32[2,192,128]{2,1,0:T(8,128)} %get-tuple-element.43), channel_id=1, source_target_pairs={{0,12},{1,13},{2,14},{3,15},{4,8},{5,9},{6,10},{7,11},{8,4},{9,5},... | collective-permute-start | bytes 589832 | tf_op jit(solution)/shard_map/ppermute | solution.py:691
  531.4 35.1 %collective-permute-start.14 = (f32[2,192,128]{2,1,0:T(8,128)}, f32[2,192,128]{2,1,0:T(8,128)S(1)}, u32[]{:S(2)}, u32[]{:S(2)}) collective-permute-start(f32[2,192,128]{2,1,0:T(8,128)} %get-tuple-element.44), channel_id=1, source_target_pairs={{0,13},{1,12},{2,15},{3,14},{4,9},{5,8},{6,11},{7,10},{8,5},{9,4},... | collective-permute-start | bytes 589832 | tf_op jit(solution)/shard_map/ppermute | solution.py:691
  533.5 38.2 %collective-permute-start.15 = (f32[2,192,128]{2,1,0:T(8,128)}, f32[2,192,128]{2,1,0:T(8,128)S(1)}, u32[]{:S(2)}, u32[]{:S(2)}) collective-permute-start(f32[2,192,128]{2,1,0:T(8,128)} %get-tuple-element.45), channel_id=1, source_target_pairs={{0,14},{1,15},{2,12},{3,13},{4,10},{5,11},{6,8},{7,9},{8,6},{9,7},... | collective-permute-start | bytes 589832 | tf_op jit(solution)/shard_map/ppermute | solution.py:691
  533.9 42.0 %collective-permute-start.16 = (f32[2,192,128]{2,1,0:T(8,128)}, f32[2,192,128]{2,1,0:T(8,128)S(1)}, u32[]{:S(2)}, u32[]{:S(2)}) collective-permute-start(f32[2,192,128]{2,1,0:T(8,128)} %get-tuple-element.46), channel_id=1, source_target_pairs={{0,15},{1,14},{2,13},{3,12},{4,11},{5,10},{6,9},{7,8},{8,7},{9,6},... | collective-permute-start | bytes 589832 | tf_op jit(solution)/shard_map/ppermute | solution.py:691
  (44 other events, 2504.8 us)
